TPU v7x, 128 devices: a whole 4x4x4 slice. The times are simulated.
128 devices in a mesh: node: 32 (over z, y_lo, x), rep: 4 (over y_hi, core).
Axes of the slice: x: 4, y: 4 (y_hi: 2, y_lo: 2; y = y_hi * 2 + y_lo), z: 4, core: 2. Of those that a mesh axis runs over, the one named last changes fastest.
Arguments:
- node_feats: bfloat16 [65536, 256], P('node'), may hold values from -6 to 6
- weight: bfloat16 [256, 256], replicated, may hold values from -0.375 to 0.375
- cotangent: bfloat16 [65536, 256], P(('node', 'rep')), may hold values from -6 to 6
- tiles: bfloat16 [32, 4, 160, 256, 256], P('node', 'rep'), may hold values from -0.049804688 to 0.049804688
- tile_rows: int32 [32, 4, 160], P('node', 'rep'), may hold values from 0 to 7
- tile_cols: int32 [32, 4, 160], P('node', 'rep'), may hold values from 0 to 63
- tile_count: int32 [32, 4], P('node', 'rep'), may hold values from 80 to 160, as said below
Outputs:
- activated: bfloat16 [65536, 256], P(('node', 'rep'))
- feature_grad: bfloat16 [65536, 256], P(('node', 'rep'))
- weight_grad: float32 [256, 256], replicated
Inputs may be any that keep to these rules, and one draw needn't show every extreme that they name: `tile_count`: slots at and beyond a device's count are ignored; some device has all 160 slots live in every draw.
All inputs are finite; a program needn't handle non-finite values.
Results may differ from a plain program's by a relative error of at most 0.007.
Values may be sent and summed in bfloat16 or wider, within the bound.
No kernel may reach another device: no remote copies, remote signals or barrier semaphores. Data moves between devices by JAX's collectives and lax.ppermute only.
A program may use at most 256 MiB of HBM per device.

v0:
```python
import jax
import jax.numpy as jnp
from jax import lax
from jax.sharding import PartitionSpec as P


def body(node_feats, weight, cotangent, tiles, tile_rows, tile_cols, tile_count):
    nrep = lax.axis_size("rep")
    nnode = lax.axis_size("node")
    rep_idx = lax.axis_index("rep")
    rows, feat = node_feats.shape
    block = tiles.shape[-1]
    row_blocks = rows // block
    quarter = row_blocks // nrep
    share = rows // nrep
    compact_cols = quarter * nnode
    slot_tiles = tiles[0, 0]
    slot_rows = tile_rows[0, 0]
    slot_cols = tile_cols[0, 0]
    slot_total = slot_tiles.shape[0]
    live = jnp.arange(slot_total, dtype=jnp.int32) < tile_count[0, 0]
    live_scale = live.astype(jnp.float32)[:, None, None]
    feat_blocks = node_feats.reshape(row_blocks, block, feat)
    mine = lax.dynamic_slice_in_dim(feat_blocks, rep_idx * quarter, quarter, 0)
    compact = lax.all_gather(mine, "node", axis=0, tiled=True)
    picked = compact[slot_cols]
    forward_prod = (
        jnp.einsum("tab,tbf->taf", slot_tiles, picked, preferred_element_type=jnp.float32)
        * live_scale
    )
    partial_agg = (
        jnp.zeros((row_blocks, block, feat), jnp.float32)
        .at[slot_rows]
        .add(forward_prod)
        .reshape(rows, feat)
    )
    scale = float(rows * nnode) ** (-0.5)
    aggregated = lax.psum(partial_agg, "rep").astype(jnp.bfloat16)
    cot_full = lax.all_gather(cotangent, "rep", axis=0, tiled=True)
    pre = jnp.dot(aggregated, weight, preferred_element_type=jnp.float32)
    sig = jax.nn.sigmoid(pre)
    activated_full = (pre * sig).astype(jnp.bfloat16)
    dpre = (cot_full.astype(jnp.float32) * sig * (1.0 + pre * (1.0 - sig))).astype(jnp.bfloat16)
    dagg = jnp.dot(dpre, weight.T, preferred_element_type=jnp.float32).astype(jnp.bfloat16)
    activated = lax.dynamic_slice_in_dim(activated_full, rep_idx * share, share, 0)
    agg_share = lax.dynamic_slice_in_dim(aggregated, rep_idx * share, share, 0)
    dpre_share = lax.dynamic_slice_in_dim(dpre, rep_idx * share, share, 0)
    weight_term = lax.dot_general(
        agg_share, dpre_share, (((0,), (0,)), ((), ())), preferred_element_type=jnp.float32
    )
    weight_grad = lax.psum(weight_term, ("node", "rep")) * scale
    dagg_blocks = dagg.reshape(row_blocks, block, feat)
    backward_prod = (
        jnp.einsum(
            "tab,taf->tbf", slot_tiles, dagg_blocks[slot_rows], preferred_element_type=jnp.float32
        )
        * live_scale
    )
    column_part = (
        jnp.zeros((compact_cols, block, feat), jnp.float32).at[slot_cols].add(backward_prod)
    )
    owned = lax.psum_scatter(column_part, "node", scatter_dimension=0, tiled=True)
    feature_grad = owned.reshape(quarter * block, feat).astype(jnp.bfloat16)
    return (activated, feature_grad, weight_grad)


def solution(mesh):
    placed = (
        P("node", None),
        P(),
        P(("node", "rep"), None),
        P("node", "rep", None, None, None),
        P("node", "rep", None),
        P("node", "rep", None),
        P("node", "rep"),
    )
    return jax.shard_map(
        body,
        mesh=mesh,
        in_specs=placed,
        out_specs=(P(("node", "rep"), None), P(("node", "rep"), None), P()),
        check_vma=False,
    )
```

profile of v0, /device:TPU:0, one launch (start us, length us, event | category | flops | bytes accessed | tf_op | source)
XLA Modules:
  0.0 760.7 jit_solution(5284792371590088112)
XLA Ops:
  7.2 0.0 copy-start
  7.2 0.0 all-gather.3.cloned.1.call-start
  7.2 1.2 copy-done
  8.4 0.7 constant_dynamic-slice_fusion
  9.1 0.0 all-gather.3.cloned.1.call-update
  9.1 0.0 all-gather.5.cloned.1.call-start
  9.2 0.7 all-gather.5.cloned.1.call-update
  9.9 0.0 all-reduce.3.cloned.1.call-start
  9.9 0.7 compare_select_fusion
  10.6 0.0 copy-start.4
  11.3 0.7 compare_select_fusion.1
  12.0 167.9 %all-gather.3.cloned.1.call-done = bf16[64,256,256]{2,1,0:T(8,128)(2,1)} async-done(((bf16[2,256,256]{2,1,0:T(8,128)(2,1)}), bf16[64,256,256]{2,1,0:T(8,128)(2,1)}) %all-gather.3.cloned.1.call-update) | async-done | bytes 8388624 | tf_op jit(solution)/shard_map/all_gather | solution.py:25
  179.9 13.0 %gather_fusion = bf16[160,256,256]{2,1,0:T(8,128)(2,1)} fusion(bf16[64,256,256]{2,1,0:T(8,128)(2,1)} %all-gather.3.cloned.1.call-done, s32[1024]{0:T(1024)S(1)} %pad_clamp_fusion.1), kind=kCustom, calls=%fused_computation | custom fusion | bytes 41943680 | tf_op jit(solution)/shard_map/gather | solution.py:26
  192.9 0.0 copy-done.4
  192.9 30.3 %multiply_bitcast_fusion.1 = f32[160,256,256]{1,2,0:T(8,128)} fusion(f32[160]{0:T(256)S(1)} %compare_convert_fusion, bf16[160,256,256]{2,1,0:T(8,128)(2,1)} %gather_fusion, bf16[1,1,160,256,256]{4,3,2,1,0:T(8,128)(2,1)} %param.10), kind=kOutput, calls=%fused_computation.5 | convolution fusion | flops 5379194880 | bytes 83886720 | tf_op jit(solution)/shard_map/tab,tbf->taf/dot_general | solution.py:28
  223.2 41.6 %copy.17 = f32[160,256,256]{2,1,0:T(8,128)} copy(f32[160,256,256]{1,2,0:T(8,128)} %multiply_bitcast_fusion.1) | data formatting | bytes 83886080 | tf_op jit(solution)/shard_map/mul | solution.py:28
  264.8 0.2 broadcast_in_dim.4
  265.0 0.0 copy-start.3
  265.0 56.6 %scatter_fusion = f32[8,256,256]{2,1,0:T(8,128)S(1)} fusion(f32[8,256,256]{2,1,0:T(8,128)S(1)} %broadcast_in_dim.4, s32[160]{0:T(256)S(1)} %bitcast.38, f32[160,256,256]{2,1,0:T(8,128)} %copy.17), kind=kCustom, calls=%fused_computation.2 | custom fusion | flops 10485760 | bytes 125829760 | tf_op jit(solution)/shard_map/scatter-add | solution.py:34
  321.6 42.6 %all-reduce.4 = bf16[2048,256]{1,0:T(8,128)(2,1)S(1)} all-reduce(f32[2048,256]{1,0:T(8,128)S(1)} %bitcast.32), channel_id=1, replica_groups=mesh['node'=32,'rep'=4] {'rep'}, use_global_device_ids=true, to_apply=%region_1.0 | all-reduce | flops 524288 | bytes 3145728 | tf_op jit(solution)/shard_map/psum | solution.py:38
  364.2 0.0 copy-start.2
  364.2 0.0 all-gather.5.cloned.1.call-done
  364.2 0.0 copy-done.3
  364.3 3.8 multiply_convert_fusion
  368.0 0.0 copy-done.2
  368.0 0.5 convolution_convert_fusion
  368.5 1.9 fusion.9
  370.4 0.0 all-reduce.3.cloned.1.call-update
  370.4 0.2 reduce-scatter.2.cloned.1.call-start
  370.7 9.5 %gather_fusion.1 = bf16[160,256,256]{2,1,0:T(8,128)(2,1)} fusion(bf16[8,256,256]{2,1,0:T(8,128)(2,1)S(1)} %bitcast.33, s32[1024]{0:T(1024)S(1)} %pad_clamp_fusion), kind=kCustom, calls=%fused_computation.1 | custom fusion | bytes 41943680 | tf_op jit(solution)/shard_map/gather | solution.py:55
  380.2 26.6 %multiply_bitcast_fusion = f32[160,256,256]{1,2,0:T(8,128)} fusion(f32[160]{0:T(256)S(1)} %compare_convert_fusion, bf16[160,256,256]{2,1,0:T(8,128)(2,1)} %gather_fusion.1, bf16[1,1,160,256,256]{4,3,2,1,0:T(8,128)(2,1)} %param.10), kind=kOutput, calls=%fused_computation.4 | convolution fusion | flops 5379194880 | bytes 83886720 | tf_op jit(solution)/shard_map/tab,taf->tbf/dot_general | solution.py:54
  406.8 0.0 copy-start.5
  406.8 41.7 %copy.19 = f32[160,256,256]{2,1,0:T(8,128)} copy(f32[160,256,256]{1,2,0:T(8,128)} %multiply_bitcast_fusion) | data formatting | bytes 83886080 | tf_op jit(solution)/shard_map/mul | solution.py:54
  448.5 7.8 %broadcast_in_dim.5 = f32[64,256,256]{2,1,0:T(8,128)} broadcast(f32[]{:T(128)} %constant.10.clone.1), dimensions={} | broadcast | bytes 16777220 | tf_op jit(solution)/shard_map/broadcast_in_dim | solution.py:60
  456.2 0.0 copy-done.5
  456.2 0.0 copy-start.1
  456.2 91.4 %scatter_fusion.1 = f32[64,256,256]{2,1,0:T(8,128)} fusion(f32[64,256,256]{2,1,0:T(8,128)} %broadcast_in_dim.5, s32[160]{0:T(256)S(1)} %bitcast.36, f32[160,256,256]{2,1,0:T(8,128)} %copy.19), kind=kCustom, calls=%fused_computation.3 | custom fusion | flops 10485760 | bytes 125829760 | tf_op jit(solution)/shard_map/scatter-add | solution.py:60
  547.7 0.0 reduce-scatter.2.cloned.1.call-update
  547.7 1.8 fusion.8
  549.5 0.0 all-reduce.3.cloned.1.call-done
  549.5 1.7 broadcast_multiply_fusion
  551.2 201.2 %reduce-scatter.2.cloned.1.call-done = f32[2,256,256]{2,1,0:T(8,128)} async-done(((f32[64,256,256]{2,1,0:T(8,128)}), f32[2,256,256]{2,1,0:T(8,128)}) %reduce-scatter.2.cloned.1.call-update) | async-done | bytes 524304 | tf_op jit(solution)/shard_map/reduce_scatter | solution.py:62
  752.4 1.8 convert_element_type.34
  754.1 0.0 copy-done.1
  (3 shorter events, 0.0 us)
Async XLA Ops:
  7.2 1.2 copy-start
  7.2 172.7 %all-gather.3.cloned.1.call-start = ((), (), s32[]{:S(2)}) async-start(), calls=%async_computation.1 | async-start | bytes 8650752 | tf_op jit(solution)/shard_map/all_gather | solution.py:25
  9.1 355.1 %all-gather.5.cloned.1.call-start = ((), (), s32[]{:S(2)}) async-start(), calls=%async_computation.2 | async-start | bytes 1310720 | tf_op jit(solution)/shard_map/all_gather | solution.py:39
  9.9 539.6 %all-reduce.3.cloned.1.call-start = ((), (), s32[]{:S(2)}) async-start(), calls=%async_computation.4 | async-start | bytes 524288 | tf_op jit(solution)/shard_map/psum | solution.py:51
  10.6 182.3 %copy-start.4 = (s32[160,1]{0,1:T(1,128)}, s32[160,1]{0,1:T(1,128)S(1)}, u32[]{:S(2)}) copy-start(s32[160,1]{0,1:T(1,128)S(1)} %compare_select_fusion) | copy-start | bytes 1924
  265.0 99.2 %copy-start.3 = (bf16[256,256]{1,0:T(8,128)(2,1)S(1)}, bf16[256,256]{1,0:T(8,128)(2,1)}, u32[]{:S(2)}) copy-start(bf16[256,256]{1,0:T(8,128)(2,1)} %param.8) | copy-start | bytes 393220
  364.2 3.8 copy-start.2
  370.4 381.9 %reduce-scatter.2.cloned.1.call-start = ((), (), s32[]{:S(2)}) async-start(), calls=%async_computation.3 | async-start | bytes 17301504 | tf_op jit(solution)/shard_map/reduce_scatter | solution.py:62
  406.8 49.5 %copy-start.5 = (s32[160,1]{0,1:T(1,128)S(1)}, s32[160,1]{0,1:T(1,128)}, u32[]{:S(2)}) copy-start(s32[160,1]{0,1:T(1,128)} %copy-done.4) | copy-start | bytes 1924
  456.2 297.9 %copy-start.1 = (bf16[2048,256]{1,0:T(8,128)(2,1)S(1)}, bf16[2048,256]{1,0:T(8,128)(2,1)}, u32[]{:S(2)}) copy-start(bf16[2048,256]{1,0:T(8,128)(2,1)} %param.7) | copy-start | bytes 3145732
Sparse Core Ops, SparseCore 0:
  10.2 169.6 all-gather.2
  181.6 21.7 all-gather.4
  370.6 142.5 all-reduce.2
  547.8 204.5 reduce-scatter.1
where the time goes:
time: 763 us; the launch traced here: 761 us
  waiting for transfers between devices  370 us (48%)
  other arithmetic  155 us (20%)
  local copies, waits for them, and re-layouts  116 us (15%)
  matrix products  63 us (8%)
  blocking collectives  42.6 us (6%)
  between operations  14.5 us (2%)
    reduce_scatter x1, waiting for transfers between devices, body(): lax.psum_scatter(column_part, 'node', scatter_dimension=0, tiled=True)  201 us
    all_gather x1, waiting for transfers between devices, body(): compact = lax.all_gather(mine, 'node', axis=0, tiled=True)  168 us
    scatter-add x1, other arithmetic, body(): jnp.zeros((compact_cols, block, feat), jnp.float32).at[slot_cols]  91.4 us
    scatter-add x1, other arithmetic, body(): partial_agg = jnp.zeros((row_blocks, block, feat), jnp.float32).at[slot_r...  56.6 us
    psum x1, blocking collectives, body(): aggregated = lax.psum(partial_agg, 'rep').astype(jnp.bfloat16)  42.6 us
    mul x1, local copies, waits for them, and re-layouts, body(): jnp.einsum('tab,taf->tbf', slot_tiles, dagg_blocks[slot_rows], preferred_...  41.7 us
    mul x1, local copies, waits for them, and re-layouts, body(): jnp.einsum('tab,tbf->taf', slot_tiles, picked, preferred_element_type=jnp...  41.6 us
    dot_general x1, matrix products, body(): jnp.einsum('tab,tbf->taf', slot_tiles, picked, preferred_element_type=jnp...  30.3 us
  transfers between devices with their start and end apart: 4, of which 2 were waited for; matrix products, arithmetic and copies ran while one was open for 43% of the time, Pallas kernels for 0%

commit v1 on v0

v1 whole, which is shorter than its diff:
```python
import functools

import jax
import jax.numpy as jnp
from jax import lax
from jax.experimental import pallas as pl
from jax.experimental.pallas import tpu as pltpu
from jax.sharding import PartitionSpec as P

AXES = ("node", "rep")
NZ, NYL, NX, NYH, NC = 4, 2, 4, 2, 2
B = 256
F32, BF16, I32 = jnp.float32, jnp.bfloat16, jnp.int32
NBUF = 8
MIB = 1 << 20


def _flat(z, yl, x, yh, c):
    return ((((z % NZ) * NYL + yl) * NX + x % NX) * NYH + yh) * NC + c


def _perm(dz=0, dyl=0, dx=0, dyh=0, dc=0):
    pairs = []
    for z in range(NZ):
        for yl in range(NYL):
            for x in range(NX):
                for yh in range(NYH):
                    for c in range(NC):
                        pairs.append(
                            (
                                _flat(z, yl, x, yh, c),
                                _flat(z + dz, yl ^ dyl, x + dx, yh ^ dyh, c ^ dc),
                            )
                        )
    return pairs


XP, XM, ZP, ZM = _perm(dx=1), _perm(dx=-1), _perm(dz=1), _perm(dz=-1)
YN, YH, CC = _perm(dyl=1), _perm(dyh=1), _perm(dc=1)


def send(value, pairs):
    return lax.ppermute(value, AXES, pairs)


def _sorted(v):
    n = v.shape[0]
    rank = jnp.sum((v[None, :] < v[:, None]).astype(I32), axis=1)
    hit = rank[:, None] == jnp.arange(n, dtype=I32)[None, :]
    return jnp.sum(jnp.where(hit, v[:, None], 0), axis=0)


def tables(rows, cols, count, z, yl, x, yh, c):
    slots = jnp.arange(rows.shape[0], dtype=I32)
    j = cols % 2
    xr = (cols // 2 % NX - x) % NX
    yr = (cols // (2 * NX) % NYL) ^ yl
    zr = (cols // (2 * NX * NYL) - z) % NZ
    near = lambda r: jnp.where(r == 0, 0, jnp.where(r == 3, 1, jnp.where(r == 1, 2, 3)))
    outer = jnp.where(j == 0, zr, xr)
    inner = jnp.where(j == 0, xr, zr)
    chunk = jnp.where(outer == 0, 0, jnp.where(outer == 2, 2, 1))
    place = near(inner) * 2 + yr
    wide = j * 16 + jnp.where(outer == 3, 0, 8) + place
    fidx = jnp.where(chunk == 1, wide, j * 8 + place)
    q = rows // 2
    rpos = ((q % 2) ^ c) * 4 + ((q // 2) ^ yh) * 2 + rows % 2
    chunk = jnp.where(slots < count, chunk, 3)
    fwd = _sorted((chunk << 24) | (rpos << 18) | (fidx << 8) | slots)
    bwd = _sorted((chunk << 24) | (fidx << 18) | (rpos << 8) | slots)
    offs = jnp.sum((chunk[None, :] < jnp.arange(4, dtype=I32)[:, None]).astype(I32), axis=1)
    return fwd, bwd, offs


def _tile_loop(tab, first, count, tiles, tbuf, tsem, step, unroll):
    def fetch(i):
        slot = tab[first + i] & 255
        at = lax.rem(i, NBUF)
        return pltpu.make_async_copy(tiles.at[slot], tbuf.at[at], tsem.at[at])

    def prime(i, carry):
        fetch(i).start()
        return carry

    def run(base, width):
        for u in range(width):
            fetch(base + u).wait()
        for u in range(width):
            i = base + u
            step(tab[first + i], tbuf.at[lax.rem(i, NBUF)])
        for u in range(width):
            i = base + u

            @pl.when(i + NBUF < count)
            def _():
                fetch(i + NBUF).start()

    whole = count // unroll

    def body():
        def many(g, carry):
            run(g * unroll, unroll)
            return carry

        def one(i, carry):
            run(i, 1)
            return carry

        lax.fori_loop(0, whole, many, 0)
        lax.fori_loop(whole * unroll, count, one, 0)

    return lambda: lax.fori_loop(0, jnp.minimum(count, NBUF), prime, 0), body


def _forward_kernel(chunk, nbuf, last, tab, offs, tiles, *refs):
    bufs, refs = refs[:nbuf], refs[nbuf:]
    if chunk:
        acc_in, refs = refs[0], refs[1:]
    outs, (feats, acc, tbuf, tsem, fsem, asem) = refs[:-6], refs[-6:]
    first = offs[chunk]
    count = offs[chunk + 1] - first

    def step(word, tile):
        r = (word >> 18) & 7
        f = (word >> 8) & 31
        acc[r] += jnp.dot(tile[...], feats[f], preferred_element_type=F32)

    prime, body = _tile_loop(tab, first, count, tiles, tbuf, tsem, step, 2)
    prime()
    copies = []
    at = 0
    for k, b in enumerate(bufs):
        n = b.shape[0]
        copies.append(pltpu.make_async_copy(b, feats.at[pl.ds(at, n)], fsem.at[k]))
        at += n
    if chunk:
        copies.append(pltpu.make_async_copy(acc_in, acc, asem))
    for cp in copies:
        cp.start()
    if not chunk:
        acc[...] = jnp.zeros_like(acc)
    for cp in copies:
        cp.wait()
    body()
    if last:
        half = acc.shape[0] // 2
        outcp = [
            pltpu.make_async_copy(acc.at[pl.ds(0, half)], outs[0], fsem.at[0]),
            pltpu.make_async_copy(acc.at[pl.ds(half, half)], outs[1], fsem.at[1]),
        ]
    else:
        outcp = [pltpu.make_async_copy(acc, outs[0], asem)]
    for cp in outcp:
        cp.start()
    for cp in outcp:
        cp.wait()


ANY = pl.BlockSpec(memory_space=pl.ANY)
SMEM = pl.BlockSpec(memory_space=pltpu.SMEM)
VMEM = pl.BlockSpec(memory_space=pltpu.VMEM)


def forward(chunk, tab, offs, tiles, bufs, acc, share):
    nblk = sum(b.shape[0] for b in bufs)
    last = chunk == 2
    full = jax.ShapeDtypeStruct((8, B, B), F32)
    half = jax.ShapeDtypeStruct((4, B, B), F32)
    outs = [half, half] if last else [full]
    args = [tab, offs, tiles, *bufs] + ([acc] if chunk else [])
    work = int(160 * share)
    res = pl.pallas_call(
        functools.partial(_forward_kernel, chunk, len(bufs), last),
        name=f"tiles_forward_{chunk}",
        in_specs=[SMEM, SMEM] + [ANY] * (len(args) - 2),
        out_specs=[ANY] * len(outs),
        out_shape=outs,
        scratch_shapes=[
            pltpu.VMEM((nblk, B, B), BF16),
            pltpu.VMEM((8, B, B), F32),
            pltpu.VMEM((NBUF, B, B), BF16),
            pltpu.SemaphoreType.DMA((NBUF,)),
            pltpu.SemaphoreType.DMA((max(2, len(bufs)),)),
            pltpu.SemaphoreType.DMA,
        ],
        compiler_params=pltpu.CompilerParams(vmem_limit_bytes=16 * MIB),
        cost_estimate=pl.CostEstimate(
            flops=work * 2 * B**3, bytes_accessed=work * B * B * 2 + 6 * MIB, transcendentals=0
        ),
    )(*args)
    return res if last else res[0]


def _backward_kernel(chunk, nout, tab, offs, tiles, d0, d1, *refs):
    outs, (dagg, acc, stage, tbuf, tsem, dsem, osem) = refs[:nout], refs[nout:]
    first = offs[chunk]
    count = offs[chunk + 1] - first

    def step(word, tile):
        f = (word >> 18) & 31
        r = (word >> 8) & 7
        acc[f] += jnp.dot(dagg[r], tile[...], preferred_element_type=F32)

    prime, body = _tile_loop(tab, first, count, tiles, tbuf, tsem, step, 2)
    prime()
    copies = [
        pltpu.make_async_copy(d0, dagg.at[pl.ds(0, 4)], dsem.at[0]),
        pltpu.make_async_copy(d1, dagg.at[pl.ds(4, 4)], dsem.at[1]),
    ]
    for cp in copies:
        cp.start()
    acc[...] = jnp.zeros_like(acc)
    for cp in copies:
        cp.wait()
    body()
    at = 0
    writes = []
    for k, o in enumerate(outs):
        n = o.shape[0]
        for m in range(n):
            stage[at + m] = acc[at + m].astype(BF16)
        cp = pltpu.make_async_copy(stage.at[pl.ds(at, n)], o, osem.at[k])
        cp.start()
        writes.append(cp)
        at += n
    for cp in writes:
        cp.wait()


def backward(chunk, tab, offs, tiles, d0, d1, sizes, share):
    nblk = sum(sizes)
    work = int(160 * share)
    return pl.pallas_call(
        functools.partial(_backward_kernel, chunk, len(sizes)),
        name=f"tiles_backward_{chunk}",
        in_specs=[SMEM, SMEM] + [ANY] * 3,
        out_specs=[ANY] * len(sizes),
        out_shape=[jax.ShapeDtypeStruct((n, B, B), BF16) for n in sizes],
        scratch_shapes=[
            pltpu.VMEM((8, B, B), BF16),
            pltpu.VMEM((nblk, B, B), F32),
            pltpu.VMEM((nblk, B, B), BF16),
            pltpu.VMEM((NBUF, B, B), BF16),
            pltpu.SemaphoreType.DMA((NBUF,)),
            pltpu.SemaphoreType.DMA((2,)),
            pltpu.SemaphoreType.DMA((len(sizes),)),
        ],
        compiler_params=pltpu.CompilerParams(vmem_limit_bytes=24 * MIB),
        cost_estimate=pl.CostEstimate(
            flops=work * 2 * B**3, bytes_accessed=work * B * B * 2 + 6 * MIB, transcendentals=0
        ),
    )(tab, offs, tiles, d0, d1)


def _dense_kernel(mine, core, far, cot0, cot1, w_ref, act, dagg, wterm):
    w = w_ref[...]
    for k in range(4):
        agg = (mine[k] + core[k] + far[(k + 2) % 4].astype(F32)).astype(BF16)
        pre = jnp.dot(agg, w, preferred_element_type=F32)
        sig = jax.nn.sigmoid(pre)
        cot = (cot0 if k < 2 else cot1)[k % 2].astype(F32)
        dpre = (cot * sig * (1.0 + pre * (1.0 - sig))).astype(BF16)
        dagg[k] = lax.dot_general(
            w, dpre, (((1,), (1,)), ((), ())), preferred_element_type=F32
        ).astype(BF16)
        if k < 2:
            act[k] = (pre * sig).astype(BF16)
            term = lax.dot_general(
                agg, dpre, (((0,), (0,)), ((), ())), preferred_element_type=F32
            )
            wterm[...] = term if k == 0 else wterm[...] + term


def dense(mine, core, far, cot0, cot1, w):
    return pl.pallas_call(
        _dense_kernel,
        name="dense",
        in_specs=[VMEM] * 6,
        out_specs=[VMEM] * 3,
        out_shape=[
            jax.ShapeDtypeStruct((2, B, B), BF16),
            jax.ShapeDtypeStruct((4, B, B), BF16),
            jax.ShapeDtypeStruct((B, B), F32),
        ],
        compiler_params=pltpu.CompilerParams(vmem_limit_bytes=16 * MIB),
        cost_estimate=pl.CostEstimate(
            flops=10 * 2 * B**3, bytes_accessed=5 * MIB, transcendentals=1024 * 256
        ),
    )(mine, core, far, cot0, cot1, w)


def plus(*terms):
    total = terms[0].astype(F32)
    for t in terms[1:]:
        total = total + t.astype(F32)
    return total.astype(BF16)


def gather(own):
    other = send(own, YN)
    e0 = jnp.stack([own[0], other[0]])
    o0 = jnp.stack([own[1], other[1]])
    e_m, e_p = send(e0, XP), send(e0, XM)
    o_m, o_p = send(o0, ZP), send(o0, ZM)
    e_a, e_b = send(e_m[:1], XP), send(e_p[1:], XM)
    o_a, o_b = send(o_m[:1], ZP), send(o_p[1:], ZM)
    even = jnp.concatenate([e0, e_m, e_p, e_a, e_b])
    odd = jnp.concatenate([o0, o_m, o_p, o_a, o_b])
    em, ep = send(even, ZP), send(even, ZM)
    om, op = send(odd, XP), send(odd, XM)
    ea, eb = send(em[:4], ZP), send(ep[4:], ZM)
    oa, ob = send(om[:4], XP), send(op[4:], XM)
    return [even, odd], [em, ep, om, op], [ea, eb, oa, ob]


def body(node_feats, weight, cotangent, tiles, tile_rows, tile_cols, tile_count):
    node, rep = lax.axis_index("node"), lax.axis_index("rep")
    x, yl, z = node % NX, node // NX % NYL, node // (NX * NYL)
    c, yh = rep % NC, rep // NC
    tiles = tiles[0, 0]
    fwd, bwd, offs = tables(
        tile_rows[0, 0], tile_cols[0, 0], tile_count[0, 0], z, yl, x, yh, c
    )
    own = lax.dynamic_slice_in_dim(node_feats.reshape(8, B, B), rep * 2, 2, 0)
    cot0 = cotangent.reshape(2, B, B)
    cot1 = send(cot0, YH)
    near, mid, far = gather(own)
    acc = forward(0, fwd, offs, tiles, near, None, 0.25)
    acc = forward(1, fwd, offs, tiles, mid, acc, 0.5)
    mine, theirs = forward(2, fwd, offs, tiles, far, acc, 0.25)
    core = send(theirs, CC)
    across = send((mine + core).astype(BF16), YH)
    act, d0, term = dense(mine, core, across, cot0, cot1, weight)
    d1 = send(d0, CC)
    scale = float(node_feats.shape[0] * NZ * NYL * NX) ** (-0.5)
    weight_grad = lax.psum(term, AXES) * scale

    ea, eb, oa, ob = backward(2, bwd, offs, tiles, d0, d1, [4, 4, 4, 4], 0.25)
    ra, rb = send(ea, ZP), send(eb, ZM)
    sa, sb = send(oa, XP), send(ob, XM)
    em0, em1, ep0, ep1, om0, om1, op0, op1 = backward(
        1, bwd, offs, tiles, d0, d1, [4] * 8, 0.5
    )
    even, odd = backward(0, bwd, offs, tiles, d0, d1, [8, 8], 0.25)
    to_zp = jnp.concatenate([plus(ep0, ra), ep1])
    to_zm = jnp.concatenate([em0, plus(em1, rb)])
    to_xp = jnp.concatenate([plus(op0, sa), op1])
    to_xm = jnp.concatenate([om0, plus(om1, sb)])
    even = plus(even, send(to_zp, ZP), send(to_zm, ZM))
    odd = plus(odd, send(to_xp, XP), send(to_xm, XM))

    def inner(q, up, down):
        ca, cb = send(q[6:7], up), send(q[7:8], down)
        to_up = jnp.concatenate([plus(q[4:5], ca), q[5:6]])
        to_down = jnp.concatenate([q[2:3], plus(q[3:4], cb)])
        return q[0:2], send(to_up, up), send(to_down, down)

    ge = inner(even, XP, XM)
    go = inner(odd, ZP, ZM)
    ge = plus(*ge)
    go = plus(*go)
    other = send(jnp.stack([ge[1], go[1]]), YN)
    total = jnp.stack([ge[0], go[0]]).astype(F32) + other.astype(F32)
    feature_grad = jnp.swapaxes(total, 1, 2).astype(BF16).reshape(2 * B, B)
    return act.reshape(2 * B, B), feature_grad, weight_grad


def solution(mesh):
    placed = (
        P("node", None),
        P(),
        P(("node", "rep"), None),
        P("node", "rep", None, None, None),
        P("node", "rep", None),
        P("node", "rep", None),
        P("node", "rep"),
    )
    return jax.shard_map(
        body,
        mesh=mesh,
        in_specs=placed,
        out_specs=(P(("node", "rep"), None), P(("node", "rep"), None), P()),
        check_vma=False,
    )
```

time: 763 us -> 374 us (0.49)
  waiting for transfers between devices: 370 us -> 149 us
  other arithmetic: 155 us -> 10.4 us
  Pallas kernels: 0 us -> 94.8 us
  local copies, waits for them, and re-layouts: 116 us -> 32.1 us
  starting transfers between devices: 0.34 us -> 69.4 us
  matrix products: 63 us -> 0 us
  blocking collectives: 42.6 us -> 0 us
    reduce_scatter x1 -> x0, waiting for transfers between devices: 201 us -> none  [body(): lax.psum_scatter(column_part, 'node', scatter_dimension=0, tiled=True)]
    all_gather x2 -> x0, waiting for transfers between devices: 168 us -> none  [the longest x1 168 us: body(): compact = lax.all_gather(mine, 'node', axis=0, tiled=True)]
    scatter-add x2 -> x0, other arithmetic: 148 us -> none  [the longest x1 91.4 us: body(): jnp.zeros((compact_cols, block, feat), jnp.float32).at[slot_cols]]
    pallas_call x0 -> x7, Pallas kernels: none -> 94.8 us  [the longest x3 48.6 us: forward(): pl.pallas_call(functools.partial(_forward_kernel, chunk, len(bufs), last)...]
    psum x1, waiting for transfers between devices: 0.01 us -> 94.3 us  [body(): weight_grad = lax.psum(term, AXES) * scale]
    mul x2 -> x0, local copies, waits for them, and re-layouts: 83.3 us -> none  [the longest x1 41.7 us: body(): jnp.einsum('tab,taf->tbf', slot_tiles, dagg_blocks[slot_rows], preferred_...]
    ppermute x0 -> x38, starting transfers between devices: none -> 69.4 us  [send(): return lax.ppermute(value, AXES, pairs)]
    dot_general x5 -> x0, matrix products: 63 us -> none  [the longest x1 30.3 us: body(): jnp.einsum('tab,tbf->taf', slot_tiles, picked, preferred_element_type=jnp...]
  transfers between devices with their start and end apart: 4 -> 39, of which waited for: 2 -> 15; matrix products, arithmetic and copies ran while one was open for 43% -> 5% of each run, Pallas kernels for 0% -> 19%
where the time goes in v1:
time: 374 us; the launch traced here: 371 us
  waiting for transfers between devices  149 us (40%)
  Pallas kernels  94.8 us (25%)
  starting transfers between devices  69.4 us (19%)
  local copies, waits for them, and re-layouts  32.1 us (9%)
  between operations  15.2 us (4%)
  other arithmetic  10.4 us (3%)
    psum x1, waiting for transfers between devices, body(): weight_grad = lax.psum(term, AXES) * scale  94.3 us
    ppermute x38, starting transfers between devices, send(): return lax.ppermute(value, AXES, pairs)  69.4 us
    ppermute x38, waiting for transfers between devices, send(): return lax.ppermute(value, AXES, pairs)  54.5 us
    pallas_call x3, Pallas kernels, forward(): pl.pallas_call(functools.partial(_forward_kernel, chunk, len(bufs), last)...  48.6 us
    pallas_call x3, Pallas kernels, backward(): pl.pallas_call(functools.partial(_backward_kernel, chunk, len(sizes)), na...  44.6 us
    unnamed x21, local copies, waits for them, and re-layouts  26.9 us
  transfers between devices with their start and end apart: 39, of which 15 were waited for; matrix products, arithmetic and copies ran while one was open for 5% of the time, Pallas kernels for 19%

profile of v1, /device:TPU:0, one launch (start us, length us, event | category | flops | bytes accessed | tf_op | source)
XLA Modules:
  0.0 370.7 jit_solution(4365144007889365712)
XLA Ops:
  8.2 1.7 collective-permute-start
  9.9 1.7 constant_dynamic-update-slice_fusion.11
  11.6 4.6 %collective-permute-done = bf16[2,256,256]{2,1,0:T(8,128)(2,1)S(1)} collective-permute-done((bf16[2,256,256]{2,1,0:T(8,128)(2,1)S(1)}, bf16[2,256,256]{2,1,0:T(8,128)(2,1)S(1)}, u32[]{:S(2)}, u32[]{:S(2)}) %collective-permute-start) | collective-permute-done | bytes 262176 | tf_op jit(solution)/shard_map/ppermute | solution.py:43
  17.0 2.1 collective-permute-start.9
  19.2 2.2 collective-permute-start.10
  21.4 1.6 collective-permute-start.1
  23.0 1.7 collective-permute-start.2
  24.7 2.0 collective-permute-done.9
  26.9 3.3 collective-permute-start.12
  30.2 1.6 collective-permute-start.3
  31.8 1.8 collective-permute-start.4
  38.1 3.0 collective-permute-start.15
  42.4 3.2 collective-permute-start.7
  46.6 14.9 %collective-permute-done.13.refs_2_ = bf16[8,256,256]{2,1,0:T(8,128)(2,1)S(1)} collective-permute-done((bf16[8,256,256]{2,1,0:T(8,128)(2,1)}, bf16[8,256,256]{2,1,0:T(8,128)(2,1)S(1)}, u32[]{:S(2)}, u32[]{:S(2)}) %collective-permute-start.13) | collective-permute-done | bytes 1048608 | tf_op jit(solution)/shard_map/ppermute | solution.py:43
  61.7 3.3 collective-permute-start.16
  67.1 3.3 collective-permute-start.8
  70.6 7.0 %copy-done = bf16[1,1,160,256,256]{4,3,2,1,0:T(8,128)(2,1)S(1)} copy-done((bf16[1,1,160,256,256]{4,3,2,1,0:T(8,128)(2,1)S(1)}, bf16[1,1,160,256,256]{4,3,2,1,0:T(8,128)(2,1)}, u32[]{:S(2)}) %copy-start) | copy-done | bytes 20971544
  77.5 10.7 %tiles_forward_0.1.refs_4_ = f32[8,256,256]{2,1,0:T(8,128)S(1)} custom-call(s32[160]{0:T(256)S(1)} %select_reduce_fusion.1.tab, s32[4]{0:T(128)S(1)} %convert_reduce_fusion.2.offs, bf16[160,256,256]{2,1,0:T(8,128)(2,1)S(1)} %bitcast.11, bf16[8,256,256]{2,1,0:T(8,128)(2,1)} %constant_dynamic-update-slice_fusion.refs_0_, ...), custom_call_target="tpu_custom_call" | custom-call | flops 1342177280 | bytes 11534336 | tf_op jit(solution)/shard_map/tiles_forward_0/pallas_call | solution.py:172
  88.3 27.1 %tiles_forward_1.1.refs_4_ = f32[8,256,256]{2,1,0:T(8,128)S(1)} custom-call(s32[160]{0:T(256)S(1)} %select_reduce_fusion.1.tab, s32[4]{0:T(128)S(1)} %convert_reduce_fusion.2.offs, bf16[160,256,256]{2,1,0:T(8,128)(2,1)S(1)} %bitcast.12, bf16[8,256,256]{2,1,0:T(8,128)(2,1)S(1)} %collective-permute-done.5.refs_0_, ...), custom_call_target="tpu_custom_call" | custom-call | flops 2684354560 | bytes 16777216 | tf_op jit(solution)/shard_map/tiles_forward_1/pallas_call | solution.py:172
  115.4 10.8 %tiles_forward_2.1 = (f32[4,256,256]{2,1,0:T(8,128)S(1)}, f32[4,256,256]{2,1,0:T(8,128)S(1)}) custom-call(s32[160]{0:T(256)S(1)} %select_reduce_fusion.1.tab, s32[4]{0:T(128)S(1)} %convert_reduce_fusion.2.offs, bf16[160,256,256]{2,1,0:T(8,128)(2,1)S(1)} %bitcast.13, bf16[4,256,256]{2,1,0:T(8,128)(2,1)S(1)} %collective-permute-done.6.refs_0_, ...), custom_call_target="tpu_custom_call" | custom-call | flops 1342177280 | bytes 11534336 | tf_op jit(solution)/shard_map/tiles_forward_2/pallas_call | solution.py:172
  126.3 1.2 collective-permute-start.17
  127.5 2.3 collective-permute-done.17.core
  130.1 3.5 collective-permute-start.19
  133.6 17.8 %collective-permute-done.19.cot1 = bf16[2,256,256]{2,1,0:T(8,128)(2,1)S(1)} collective-permute-done((bf16[2,256,256]{2,1,0:T(8,128)(2,1)S(1)}, bf16[2,256,256]{2,1,0:T(8,128)(2,1)S(1)}, u32[]{:S(2)}, u32[]{:S(2)}) %collective-permute-start.19) | collective-permute-done | bytes 262176 | tf_op jit(solution)/shard_map/ppermute | solution.py:43
  151.4 1.6 dense.1
  153.3 1.6 collective-permute-done.20.d1
  154.9 7.0 %copy-done.1 = bf16[1,1,160,256,256]{4,3,2,1,0:T(8,128)(2,1)S(1)} copy-done((bf16[1,1,160,256,256]{4,3,2,1,0:T(8,128)(2,1)S(1)}, bf16[1,1,160,256,256]{4,3,2,1,0:T(8,128)(2,1)}, u32[]{:S(2)}) %copy-start.1) | copy-done | bytes 20971544
  161.8 10.5 %tiles_backward_2.1 = (bf16[4,256,256]{2,1,0:T(8,128)(2,1)S(1)}, bf16[4,256,256]{2,1,0:T(8,128)(2,1)S(1)}, bf16[4,256,256]{2,1,0:T(8,128)(2,1)S(1)}, bf16[4,256,256]{2,1,0:T(8,128)(2,1)S(1)}) custom-call(s32[160]{0:T(256)S(1)} %select_reduce_fusion.tab, s32[4]{0:T(128)S(1)} %convert_reduce_fusion.2.offs, bf16[160,256,256]{2,1,0:T(8,128)(2,1)S(1)} %bitcast.14, ...), custom_call_target="tpu_custom_call" | custom-call | flops 1342177280 | bytes 11534336 | tf_op jit(solution)/shard_map/tiles_backward_2/pallas_call | solution.py:233
  172.5 3.1 collective-permute-start.23
  175.7 6.8 %collective-permute-start.29 = (bf16[4,256,256]{2,1,0:T(8,128)(2,1)S(1)}, bf16[4,256,256]{2,1,0:T(8,128)(2,1)S(1)}, u32[]{:S(2)}, u32[]{:S(2)}) collective-permute-start(bf16[4,256,256]{2,1,0:T(8,128)(2,1)S(1)} %get-tuple-element.35), channel_id=1, source_target_pairs={{0,4},{1,5},{2,6},{3,7},{4,8},{5,9},{6,10},{7,11},{8,12},{9,13},{1... | collective-permute-start | bytes 1572872 | tf_op jit(solution)/shard_map/ppermute | solution.py:43
  182.5 25.0 %tiles_backward_1.1 = (bf16[4,256,256]{2,1,0:T(8,128)(2,1)S(1)}, bf16[4,256,256]{2,1,0:T(8,128)(2,1)S(1)}, bf16[4,256,256]{2,1,0:T(8,128)(2,1)S(1)}, bf16[4,256,...) custom-call(s32[160]{0:T(256)S(1)} %select_reduce_fusion.tab, ...), custom_call_target="tpu_custom_call" | custom-call | flops 2684354560 | bytes 16777216 | tf_op jit(solution)/shard_map/tiles_backward_1/pallas_call | solution.py:233
  210.0 3.2 collective-permute-start.24
  214.4 6.6 %collective-permute-start.30 = (bf16[8,256,256]{2,1,0:T(8,128)(2,1)}, bf16[8,256,256]{2,1,0:T(8,128)(2,1)}, u32[]{:S(2)}, u32[]{:S(2)}) collective-permute-start(bf16[8,256,256]{2,1,0:T(8,128)(2,1)} %pad_maximum_fusion.2), channel_id=1, source_target_pairs={{0,4},{1,5},{2,6},{3,7},{4,8},{5,9},{6,10},{7,11},{8,12},{9,13},{1... | collective-permute-start | bytes 3145736 | tf_op jit(solution)/shard_map/ppermute | solution.py:43
  221.4 7.0 %copy-done.2 = bf16[1,1,160,256,256]{4,3,2,1,0:T(8,128)(2,1)S(1)} copy-done((bf16[1,1,160,256,256]{4,3,2,1,0:T(8,128)(2,1)S(1)}, bf16[1,1,160,256,256]{4,3,2,1,0:T(8,128)(2,1)}, u32[]{:S(2)}) %copy-start.2) | copy-done | bytes 20971544
  228.4 9.1 %tiles_backward_0.1 = (bf16[8,256,256]{2,1,0:T(8,128)(2,1)S(1)}, bf16[8,256,256]{2,1,0:T(8,128)(2,1)S(1)}) custom-call(s32[160]{0:T(256)S(1)} %select_reduce_fusion.tab, s32[4]{0:T(128)S(1)} %convert_reduce_fusion.2.offs, bf16[160,256,256]{2,1,0:T(8,128)(2,1)S(1)} %bitcast.16, bf16[4,256,256]{2,1,0:T(8,128)(2,1)S(1)} %get-tuple-element.25.d0, ...), custom_call_target="tpu_custom_call" | custom-call | flops 1342177280 | bytes 11534336 | tf_op jit(solution)/shard_map/tiles_backward_0/pallas_call | solution.py:233
  238.0 3.9 %collective-permute-done.32 = bf16[8,256,256]{2,1,0:T(8,128)(2,1)} collective-permute-done((bf16[8,256,256]{2,1,0:T(8,128)(2,1)S(1)}, bf16[8,256,256]{2,1,0:T(8,128)(2,1)}, u32[]{:S(2)}, u32[]{:S(2)}) %collective-permute-start.32) | collective-permute-done | bytes 1048608 | tf_op jit(solution)/shard_map/ppermute | solution.py:43
  241.9 3.2 add_convert_fusion
  245.1 2.2 collective-permute-start.25
  247.3 1.1 collective-permute-start.27
  248.6 3.2 collective-permute-start.35
  252.4 1.2 collective-permute-done.27
  253.7 2.0 collective-permute-start.26
  255.7 1.4 collective-permute-start.28
  257.3 3.3 collective-permute-start.36
  262.4 2.6 collective-permute-done.34
  265.1 1.8 collective-permute-start.37
  267.0 94.3 %all-reduce.2.cloned.1.call-done = f32[256,256]{1,0:T(8,128)} async-done(((f32[256,256]{1,0:T(8,128)}), f32[256,256]{1,0:T(8,128)}) %all-reduce.2.cloned.1.call-update) | async-done | bytes 262160 | tf_op jit(solution)/shard_map/psum | solution.py:336
  361.2 1.7 broadcast_multiply_fusion
  (107 shorter events, 19.8 us)
Async XLA Ops:
  7.2 354.1 %all-reduce.2.cloned.1.call-start = ((), (), s32[]{:S(2)}) async-start(), calls=%async_computation | async-start | bytes 524288 | tf_op jit(solution)/shard_map/psum | solution.py:336
  8.2 8.0 %collective-permute-start = (bf16[2,256,256]{2,1,0:T(8,128)(2,1)S(1)}, bf16[2,256,256]{2,1,0:T(8,128)(2,1)S(1)}, u32[]{:S(2)}, u32[]{:S(2)}) collective-permute-start(bf16[2,256,256]{2,1,0:T(8,128)(2,1)S(1)} %constant_dynamic-slice_fusion.1), channel_id=1, source_target_pairs={{0,16},{1,17},{2,18},{3,19},{4,20},{5,21},{6,22},{7,23},{8,24},{9,... | collective-permute-start | bytes 786440 | tf_op jit(solution)/shard_map/ppermute | solution.py:43
  17.0 9.7 %collective-permute-start.9 = (bf16[2,256,256]{2,1,0:T(8,128)(2,1)S(1)}, bf16[2,256,256]{2,1,0:T(8,128)(2,1)S(1)}, u32[]{:S(2)}, u32[]{:S(2)}) collective-permute-start(bf16[2,256,256]{2,1,0:T(8,128)(2,1)S(1)} %pad_maximum_fusion.5), channel_id=1, source_target_pairs={{0,32},{1,33},{2,34},{3,35},{4,36},{5,37},{6,38},{7,39},{8,40},{9,... | collective-permute-start | bytes 786440 | tf_op jit(solution)/shard_map/ppermute | solution.py:43
  19.2 7.7 %collective-permute-start.10 = (bf16[2,256,256]{2,1,0:T(8,128)(2,1)S(1)}, bf16[2,256,256]{2,1,0:T(8,128)(2,1)S(1)}, u32[]{:S(2)}, u32[]{:S(2)}) collective-permute-start(bf16[2,256,256]{2,1,0:T(8,128)(2,1)S(1)} %pad_maximum_fusion.5), channel_id=1, source_target_pairs={{0,96},{1,97},{2,98},{3,99},{4,100},{5,101},{6,102},{7,103},{8,104... | collective-permute-start | bytes 786440 | tf_op jit(solution)/shard_map/ppermute | solution.py:43
  21.4 24.9 %copy-start.5 = (s32[1,1,160]{2,1,0:T(1,128)S(1)}, s32[1,1,160]{2,1,0:T(1,128)}, u32[]{:S(2)}) copy-start(s32[1,1,160]{2,1,0:T(1,128)} %param.12) | copy-start | bytes 1924
  21.4 8.7 %collective-permute-start.1 = (bf16[2,256,256]{2,1,0:T(8,128)(2,1)S(1)}, bf16[2,256,256]{2,1,0:T(8,128)(2,1)S(1)}, u32[]{:S(2)}, u32[]{:S(2)}) collective-permute-start(bf16[2,256,256]{2,1,0:T(8,128)(2,1)S(1)} %pad_maximum_fusion.4), channel_id=1, source_target_pairs={{0,4},{1,5},{2,6},{3,7},{4,8},{5,9},{6,10},{7,11},{8,12},{9,13},{1... | collective-permute-start | bytes 786440 | tf_op jit(solution)/shard_map/ppermute | solution.py:43
  23.0 8.7 %collective-permute-start.2 = (bf16[2,256,256]{2,1,0:T(8,128)(2,1)S(1)}, bf16[2,256,256]{2,1,0:T(8,128)(2,1)S(1)}, u32[]{:S(2)}, u32[]{:S(2)}) collective-permute-start(bf16[2,256,256]{2,1,0:T(8,128)(2,1)S(1)} %pad_maximum_fusion.4), channel_id=1, source_target_pairs={{0,12},{1,13},{2,14},{3,15},{4,0},{5,1},{6,2},{7,3},{8,4},{9,5},{1... | collective-permute-start | bytes 786440 | tf_op jit(solution)/shard_map/ppermute | solution.py:43
  26.8 19.6 %copy-start.6 = (s32[1,1,160]{2,1,0:T(1,128)S(1)}, s32[1,1,160]{2,1,0:T(1,128)}, u32[]{:S(2)}) copy-start(s32[1,1,160]{2,1,0:T(1,128)} %param.11) | copy-start | bytes 1924
  26.8 9.7 %collective-permute-start.11 = (bf16[1,256,256]{2,1,0:T(8,128)(2,1)S(1)}, bf16[1,256,256]{2,1,0:T(8,128)(2,1)S(1)}, u32[]{:S(2)}, u32[]{:S(2)}) collective-permute-start(bf16[1,256,256]{2,1,0:T(8,128)(2,1)S(1)} %slice.126), channel_id=1, source_target_pairs={{0,32},{1,33},{2,34},{3,35},{4,36},{5,37},{6,38},{7,39},{8,40},{9,... | collective-permute-start | bytes 393224 | tf_op jit(solution)/shard_map/ppermute | solution.py:43
  26.9 10.3 %collective-permute-start.12 = (bf16[1,256,256]{2,1,0:T(8,128)(2,1)S(1)}, bf16[1,256,256]{2,1,0:T(8,128)(2,1)S(1)}, u32[]{:S(2)}, u32[]{:S(2)}) collective-permute-start(bf16[1,256,256]{2,1,0:T(8,128)(2,1)S(1)} %slice.127), channel_id=1, source_target_pairs={{0,96},{1,97},{2,98},{3,99},{4,100},{5,101},{6,102},{7,103},{8,104... | collective-permute-start | bytes 393224 | tf_op jit(solution)/shard_map/ppermute | solution.py:43
  30.2 10.9 %collective-permute-start.3 = (bf16[1,256,256]{2,1,0:T(8,128)(2,1)S(1)}, bf16[1,256,256]{2,1,0:T(8,128)(2,1)S(1)}, u32[]{:S(2)}, u32[]{:S(2)}) collective-permute-start(bf16[1,256,256]{2,1,0:T(8,128)(2,1)S(1)} %slice.121), channel_id=1, source_target_pairs={{0,4},{1,5},{2,6},{3,7},{4,8},{5,9},{6,10},{7,11},{8,12},{9,13},{1... | collective-permute-start | bytes 393224 | tf_op jit(solution)/shard_map/ppermute | solution.py:43
  31.8 10.0 %collective-permute-start.4 = (bf16[1,256,256]{2,1,0:T(8,128)(2,1)S(1)}, bf16[1,256,256]{2,1,0:T(8,128)(2,1)S(1)}, u32[]{:S(2)}, u32[]{:S(2)}) collective-permute-start(bf16[1,256,256]{2,1,0:T(8,128)(2,1)S(1)} %slice.122), channel_id=1, source_target_pairs={{0,12},{1,13},{2,14},{3,15},{4,0},{5,1},{6,2},{7,3},{8,4},{9,5},{1... | collective-permute-start | bytes 393224 | tf_op jit(solution)/shard_map/ppermute | solution.py:43
  37.8 23.7 %collective-permute-start.13 = (bf16[8,256,256]{2,1,0:T(8,128)(2,1)}, bf16[8,256,256]{2,1,0:T(8,128)(2,1)S(1)}, u32[]{:S(2)}, u32[]{:S(2)}) collective-permute-start(bf16[8,256,256]{2,1,0:T(8,128)(2,1)} %constant_dynamic-update-slice_fusion.6.refs_1_), channel_id=1, source_target_pairs={{0,4},{1,5},{2,6},{3,7},{4,8},{5,9},{6,10},{7,11},{8,12},{9,13},{1... | collective-permute-start | bytes 3145736 | tf_op jit(solution)/shard_map/ppermute | solution.py:43
  38.1 23.5 %collective-permute-start.15 = (bf16[8,256,256]{2,1,0:T(8,128)(2,1)}, bf16[8,256,256]{2,1,0:T(8,128)(2,1)S(1)}, u32[]{:S(2)}, u32[]{:S(2)}) collective-permute-start(bf16[8,256,256]{2,1,0:T(8,128)(2,1)} %constant_dynamic-update-slice_fusion.6.refs_1_), channel_id=1, source_target_pairs={{0,12},{1,13},{2,14},{3,15},{4,0},{5,1},{6,2},{7,3},{8,4},{9,5},{1... | collective-permute-start | bytes 3145736 | tf_op jit(solution)/shard_map/ppermute | solution.py:43
  42.4 23.4 %collective-permute-start.5 = (bf16[8,256,256]{2,1,0:T(8,128)(2,1)}, bf16[8,256,256]{2,1,0:T(8,128)(2,1)S(1)}, u32[]{:S(2)}, u32[]{:S(2)}) collective-permute-start(bf16[8,256,256]{2,1,0:T(8,128)(2,1)} %constant_dynamic-update-slice_fusion.refs_0_), channel_id=1, source_target_pairs={{0,32},{1,33},{2,34},{3,35},{4,36},{5,37},{6,38},{7,39},{8,40},{9,... | collective-permute-start | bytes 3145736 | tf_op jit(solution)/shard_map/ppermute | solution.py:43
  42.4 23.5 %collective-permute-start.7 = (bf16[8,256,256]{2,1,0:T(8,128)(2,1)}, bf16[8,256,256]{2,1,0:T(8,128)(2,1)}, u32[]{:S(2)}, u32[]{:S(2)}) collective-permute-start(bf16[8,256,256]{2,1,0:T(8,128)(2,1)} %constant_dynamic-update-slice_fusion.refs_0_), channel_id=1, source_target_pairs={{0,96},{1,97},{2,98},{3,99},{4,100},{5,101},{6,102},{7,103},{8,104... | collective-permute-start | bytes 3145736 | tf_op jit(solution)/shard_map/ppermute | solution.py:43
  61.6 53.8 %collective-permute-start.14 = (bf16[4,256,256]{2,1,0:T(8,128)(2,1)S(1)}, bf16[4,256,256]{2,1,0:T(8,128)(2,1)S(1)}, u32[]{:S(2)}, u32[]{:S(2)}) collective-permute-start(bf16[4,256,256]{2,1,0:T(8,128)(2,1)S(1)} %slice.128), channel_id=1, source_target_pairs={{0,4},{1,5},{2,6},{3,7},{4,8},{5,9},{6,10},{7,11},{8,12},{9,13},{1... | collective-permute-start | bytes 1572872 | tf_op jit(solution)/shard_map/ppermute | solution.py:43
  61.7 53.7 %collective-permute-start.16 = (bf16[4,256,256]{2,1,0:T(8,128)(2,1)S(1)}, bf16[4,256,256]{2,1,0:T(8,128)(2,1)S(1)}, u32[]{:S(2)}, u32[]{:S(2)}) collective-permute-start(bf16[4,256,256]{2,1,0:T(8,128)(2,1)S(1)} %slice.129), channel_id=1, source_target_pairs={{0,12},{1,13},{2,14},{3,15},{4,0},{5,1},{6,2},{7,3},{8,4},{9,5},{1... | collective-permute-start | bytes 1572872 | tf_op jit(solution)/shard_map/ppermute | solution.py:43
  65.9 49.5 %collective-permute-start.6 = (bf16[4,256,256]{2,1,0:T(8,128)(2,1)S(1)}, bf16[4,256,256]{2,1,0:T(8,128)(2,1)S(1)}, u32[]{:S(2)}, u32[]{:S(2)}) collective-permute-start(bf16[4,256,256]{2,1,0:T(8,128)(2,1)S(1)} %slice.123), channel_id=1, source_target_pairs={{0,32},{1,33},{2,34},{3,35},{4,36},{5,37},{6,38},{7,39},{8,40},{9,... | collective-permute-start | bytes 1572872 | tf_op jit(solution)/shard_map/ppermute | solution.py:43
  67.1 48.3 %collective-permute-start.8 = (bf16[4,256,256]{2,1,0:T(8,128)(2,1)S(1)}, bf16[4,256,256]{2,1,0:T(8,128)(2,1)S(1)}, u32[]{:S(2)}, u32[]{:S(2)}) collective-permute-start(bf16[4,256,256]{2,1,0:T(8,128)(2,1)S(1)} %slice.124), channel_id=1, source_target_pairs={{0,96},{1,97},{2,98},{3,99},{4,100},{5,101},{6,102},{7,103},{8,104... | collective-permute-start | bytes 1572872 | tf_op jit(solution)/shard_map/ppermute | solution.py:43
  70.6 7.0 %copy-start = (bf16[1,1,160,256,256]{4,3,2,1,0:T(8,128)(2,1)S(1)}, bf16[1,1,160,256,256]{4,3,2,1,0:T(8,128)(2,1)}, u32[]{:S(2)}) copy-start(bf16[1,1,160,256,256]{4,3,2,1,0:T(8,128)(2,1)} %param.10) | copy-start | bytes 62914564
  126.2 3.8 %copy-start.3 = (bf16[512,256]{1,0:T(8,128)(2,1)S(1)}, bf16[512,256]{1,0:T(8,128)(2,1)}, u32[]{:S(2)}) copy-start(bf16[512,256]{1,0:T(8,128)(2,1)} %param.9) | copy-start | bytes 786436
  126.3 25.1 %copy-start.4 = (bf16[256,256]{1,0:T(8,128)(2,1)S(1)}, bf16[256,256]{1,0:T(8,128)(2,1)}, u32[]{:S(2)}) copy-start(bf16[256,256]{1,0:T(8,128)(2,1)} %w_ref.1) | copy-start | bytes 393220
  126.3 3.5 collective-permute-start.17
  130.0 21.4 %collective-permute-start.18 = (bf16[4,256,256]{2,1,0:T(8,128)(2,1)S(1)}, bf16[4,256,256]{2,1,0:T(8,128)(2,1)S(1)}, u32[]{:S(2)}, u32[]{:S(2)}) collective-permute-start(bf16[4,256,256]{2,1,0:T(8,128)(2,1)S(1)} %add_convert_fusion.6), channel_id=1, source_target_pairs={{0,2},{1,3},{2,0},{3,1},{4,6},{5,7},{6,4},{7,5},{8,10},{9,11},{10,... | collective-permute-start | bytes 1572872 | tf_op jit(solution)/shard_map/ppermute | solution.py:43
  130.1 21.3 %collective-permute-start.19 = (bf16[2,256,256]{2,1,0:T(8,128)(2,1)S(1)}, bf16[2,256,256]{2,1,0:T(8,128)(2,1)S(1)}, u32[]{:S(2)}, u32[]{:S(2)}) collective-permute-start(bf16[2,256,256]{2,1,0:T(8,128)(2,1)S(1)} %bitcast.17), channel_id=1, source_target_pairs={{0,2},{1,3},{2,0},{3,1},{4,6},{5,7},{6,4},{7,5},{8,10},{9,11},{10,... | collective-permute-start | bytes 786440 | tf_op jit(solution)/shard_map/ppermute | solution.py:43
  153.0 1.9 collective-permute-start.20
  154.9 7.0 %copy-start.1 = (bf16[1,1,160,256,256]{4,3,2,1,0:T(8,128)(2,1)S(1)}, bf16[1,1,160,256,256]{4,3,2,1,0:T(8,128)(2,1)}, u32[]{:S(2)}) copy-start(bf16[1,1,160,256,256]{4,3,2,1,0:T(8,128)(2,1)} %param.10) | copy-start | bytes 62914564
  172.4 35.1 %collective-permute-start.21 = (bf16[4,256,256]{2,1,0:T(8,128)(2,1)S(1)}, bf16[4,256,256]{2,1,0:T(8,128)(2,1)S(1)}, u32[]{:S(2)}, u32[]{:S(2)}) collective-permute-start(bf16[4,256,256]{2,1,0:T(8,128)(2,1)S(1)} %get-tuple-element.28), channel_id=1, source_target_pairs={{0,32},{1,33},{2,34},{3,35},{4,36},{5,37},{6,38},{7,39},{8,40},{9,... | collective-permute-start | bytes 1572872 | tf_op jit(solution)/shard_map/ppermute | solution.py:43
  172.5 36.2 %collective-permute-start.23 = (bf16[4,256,256]{2,1,0:T(8,128)(2,1)S(1)}, bf16[4,256,256]{2,1,0:T(8,128)(2,1)S(1)}, u32[]{:S(2)}, u32[]{:S(2)}) collective-permute-start(bf16[4,256,256]{2,1,0:T(8,128)(2,1)S(1)} %get-tuple-element.32), channel_id=1, source_target_pairs={{0,96},{1,97},{2,98},{3,99},{4,100},{5,101},{6,102},{7,103},{8,104... | collective-permute-start | bytes 1572872 | tf_op jit(solution)/shard_map/ppermute | solution.py:43
  175.7 37.5 %collective-permute-start.29 = (bf16[4,256,256]{2,1,0:T(8,128)(2,1)S(1)}, bf16[4,256,256]{2,1,0:T(8,128)(2,1)S(1)}, u32[]{:S(2)}, u32[]{:S(2)}) collective-permute-start(bf16[4,256,256]{2,1,0:T(8,128)(2,1)S(1)} %get-tuple-element.35), channel_id=1, source_target_pairs={{0,4},{1,5},{2,6},{3,7},{4,8},{5,9},{6,10},{7,11},{8,12},{9,13},{1... | collective-permute-start | bytes 1572872 | tf_op jit(solution)/shard_map/ppermute | solution.py:43
  182.5 38.5 %collective-permute-start.31 = (bf16[4,256,256]{2,1,0:T(8,128)(2,1)S(1)}, bf16[4,256,256]{2,1,0:T(8,128)(2,1)S(1)}, u32[]{:S(2)}, u32[]{:S(2)}) collective-permute-start(bf16[4,256,256]{2,1,0:T(8,128)(2,1)S(1)} %get-tuple-element.39), channel_id=1, source_target_pairs={{0,12},{1,13},{2,14},{3,15},{4,0},{5,1},{6,2},{7,3},{8,4},{9,5},{1... | collective-permute-start | bytes 1572872 | tf_op jit(solution)/shard_map/ppermute | solution.py:43
  208.7 28.8 %collective-permute-start.22 = (bf16[8,256,256]{2,1,0:T(8,128)(2,1)}, bf16[8,256,256]{2,1,0:T(8,128)(2,1)}, u32[]{:S(2)}, u32[]{:S(2)}) collective-permute-start(bf16[8,256,256]{2,1,0:T(8,128)(2,1)} %pad_maximum_fusion), channel_id=1, source_target_pairs={{0,32},{1,33},{2,34},{3,35},{4,36},{5,37},{6,38},{7,39},{8,40},{9,... | collective-permute-start | bytes 3145736 | tf_op jit(solution)/shard_map/ppermute | solution.py:43
  210.0 27.6 %collective-permute-start.24 = (bf16[8,256,256]{2,1,0:T(8,128)(2,1)}, bf16[8,256,256]{2,1,0:T(8,128)(2,1)}, u32[]{:S(2)}, u32[]{:S(2)}) collective-permute-start(bf16[8,256,256]{2,1,0:T(8,128)(2,1)} %pad_maximum_fusion.1), channel_id=1, source_target_pairs={{0,96},{1,97},{2,98},{3,99},{4,100},{5,101},{6,102},{7,103},{8,104... | collective-permute-start | bytes 3145736 | tf_op jit(solution)/shard_map/ppermute | solution.py:43
  214.4 23.6 %collective-permute-start.30 = (bf16[8,256,256]{2,1,0:T(8,128)(2,1)}, bf16[8,256,256]{2,1,0:T(8,128)(2,1)}, u32[]{:S(2)}, u32[]{:S(2)}) collective-permute-start(bf16[8,256,256]{2,1,0:T(8,128)(2,1)} %pad_maximum_fusion.2), channel_id=1, source_target_pairs={{0,4},{1,5},{2,6},{3,7},{4,8},{5,9},{6,10},{7,11},{8,12},{9,13},{1... | collective-permute-start | bytes 3145736 | tf_op jit(solution)/shard_map/ppermute | solution.py:43
  221.3 20.7 %collective-permute-start.32 = (bf16[8,256,256]{2,1,0:T(8,128)(2,1)S(1)}, bf16[8,256,256]{2,1,0:T(8,128)(2,1)}, u32[]{:S(2)}, u32[]{:S(2)}) collective-permute-start(bf16[8,256,256]{2,1,0:T(8,128)(2,1)S(1)} %pad_maximum_fusion.3), channel_id=1, source_target_pairs={{0,12},{1,13},{2,14},{3,15},{4,0},{5,1},{6,2},{7,3},{8,4},{9,5},{1... | collective-permute-start | bytes 3145736 | tf_op jit(solution)/shard_map/ppermute | solution.py:43
  221.4 7.0 %copy-start.2 = (bf16[1,1,160,256,256]{4,3,2,1,0:T(8,128)(2,1)S(1)}, bf16[1,1,160,256,256]{4,3,2,1,0:T(8,128)(2,1)}, u32[]{:S(2)}) copy-start(bf16[1,1,160,256,256]{4,3,2,1,0:T(8,128)(2,1)} %param.10) | copy-start | bytes 62914564
  245.1 7.3 %collective-permute-start.25 = (bf16[1,256,256]{2,1,0:T(8,128)(2,1)S(1)}, bf16[1,256,256]{2,1,0:T(8,128)(2,1)S(1)}, u32[]{:S(2)}, u32[]{:S(2)}) collective-permute-start(bf16[1,256,256]{2,1,0:T(8,128)(2,1)S(1)} %get-tuple-element.51), channel_id=1, source_target_pairs={{0,4},{1,5},{2,6},{3,7},{4,8},{5,9},{6,10},{7,11},{8,12},{9,13},{1... | collective-permute-start | bytes 393224 | tf_op jit(solution)/shard_map/ppermute | solution.py:43
  247.3 6.3 %collective-permute-start.27 = (bf16[1,256,256]{2,1,0:T(8,128)(2,1)S(1)}, bf16[1,256,256]{2,1,0:T(8,128)(2,1)S(1)}, u32[]{:S(2)}, u32[]{:S(2)}) collective-permute-start(bf16[1,256,256]{2,1,0:T(8,128)(2,1)S(1)} %get-tuple-element.52), channel_id=1, source_target_pairs={{0,12},{1,13},{2,14},{3,15},{4,0},{5,1},{6,2},{7,3},{8,4},{9,5},{1... | collective-permute-start | bytes 393224 | tf_op jit(solution)/shard_map/ppermute | solution.py:43
  248.5 8.6 %collective-permute-start.33 = (bf16[1,256,256]{2,1,0:T(8,128)(2,1)S(1)}, bf16[1,256,256]{2,1,0:T(8,128)(2,1)S(1)}, u32[]{:S(2)}, u32[]{:S(2)}) collective-permute-start(bf16[1,256,256]{2,1,0:T(8,128)(2,1)S(1)} %get-tuple-element.57), channel_id=1, source_target_pairs={{0,32},{1,33},{2,34},{3,35},{4,36},{5,37},{6,38},{7,39},{8,40},{9,... | collective-permute-start | bytes 393224 | tf_op jit(solution)/shard_map/ppermute | solution.py:43
  248.6 8.5 %collective-permute-start.35 = (bf16[1,256,256]{2,1,0:T(8,128)(2,1)S(1)}, bf16[1,256,256]{2,1,0:T(8,128)(2,1)S(1)}, u32[]{:S(2)}, u32[]{:S(2)}) collective-permute-start(bf16[1,256,256]{2,1,0:T(8,128)(2,1)S(1)} %get-tuple-element.58), channel_id=1, source_target_pairs={{0,96},{1,97},{2,98},{3,99},{4,100},{5,101},{6,102},{7,103},{8,104... | collective-permute-start | bytes 393224 | tf_op jit(solution)/shard_map/ppermute | solution.py:43
  253.7 7.7 %collective-permute-start.26 = (bf16[2,256,256]{2,1,0:T(8,128)(2,1)S(1)}, bf16[2,256,256]{2,1,0:T(8,128)(2,1)S(1)}, u32[]{:S(2)}, u32[]{:S(2)}) collective-permute-start(bf16[2,256,256]{2,1,0:T(8,128)(2,1)S(1)} %pad_maximum_fusion.6), channel_id=1, source_target_pairs={{0,4},{1,5},{2,6},{3,7},{4,8},{5,9},{6,10},{7,11},{8,12},{9,13},{1... | collective-permute-start | bytes 786440 | tf_op jit(solution)/shard_map/ppermute | solution.py:43
  255.7 6.5 %collective-permute-start.28 = (bf16[2,256,256]{2,1,0:T(8,128)(2,1)S(1)}, bf16[2,256,256]{2,1,0:T(8,128)(2,1)S(1)}, u32[]{:S(2)}, u32[]{:S(2)}) collective-permute-start(bf16[2,256,256]{2,1,0:T(8,128)(2,1)S(1)} %pad_maximum_fusion.7), channel_id=1, source_target_pairs={{0,12},{1,13},{2,14},{3,15},{4,0},{5,1},{6,2},{7,3},{8,4},{9,5},{1... | collective-permute-start | bytes 786440 | tf_op jit(solution)/shard_map/ppermute | solution.py:43
  257.2 7.7 %collective-permute-start.34 = (bf16[2,256,256]{2,1,0:T(8,128)(2,1)S(1)}, bf16[2,256,256]{2,1,0:T(8,128)(2,1)S(1)}, u32[]{:S(2)}, u32[]{:S(2)}) collective-permute-start(bf16[2,256,256]{2,1,0:T(8,128)(2,1)S(1)} %pad_maximum_fusion.8), channel_id=1, source_target_pairs={{0,32},{1,33},{2,34},{3,35},{4,36},{5,37},{6,38},{7,39},{8,40},{9,... | collective-permute-start | bytes 786440 | tf_op jit(solution)/shard_map/ppermute | solution.py:43
  257.3 7.6 %collective-permute-start.36 = (bf16[2,256,256]{2,1,0:T(8,128)(2,1)S(1)}, bf16[2,256,256]{2,1,0:T(8,128)(2,1)S(1)}, u32[]{:S(2)}, u32[]{:S(2)}) collective-permute-start(bf16[2,256,256]{2,1,0:T(8,128)(2,1)S(1)} %pad_maximum_fusion.9), channel_id=1, source_target_pairs={{0,96},{1,97},{2,98},{3,99},{4,100},{5,101},{6,102},{7,103},{8,104... | collective-permute-start | bytes 786440 | tf_op jit(solution)/shard_map/ppermute | solution.py:43
  265.1 97.8 %collective-permute-start.37 = (bf16[2,256,256]{2,1,0:T(8,128)(2,1)S(1)}, bf16[2,256,256]{2,1,0:T(8,128)(2,1)S(1)}, u32[]{:S(2)}, u32[]{:S(2)}) collective-permute-start(bf16[2,256,256]{2,1,0:T(8,128)(2,1)S(1)} %pad_maximum_fusion.10), channel_id=1, source_target_pairs={{0,16},{1,17},{2,18},{3,19},{4,20},{5,21},{6,22},{7,23},{8,24},{9,... | collective-permute-start | bytes 786440 | tf_op jit(solution)/shard_map/ppermute | solution.py:43
Sparse Core Ops, SparseCore 0:
  221.5 139.6 all-reduce.1

commit v2 on v1

--- a/solution.py
+++ b/solution.py
@@ -11,7 +11,8 @@
 NZ, NYL, NX, NYH, NC = 4, 2, 4, 2, 2
 B = 256
 F32, BF16, I32 = jnp.float32, jnp.bfloat16, jnp.int32
-NBUF = 8
+NBUF = 32
+UNROLL = 8
 MIB = 1 << 20
 
 
@@ -36,11 +37,32 @@
 
 
 XP, XM, ZP, ZM = _perm(dx=1), _perm(dx=-1), _perm(dz=1), _perm(dz=-1)
+X2, Z2 = _perm(dx=2), _perm(dz=2)
 YN, YH, CC = _perm(dyl=1), _perm(dyh=1), _perm(dc=1)
+
+
+def _pairs(axis, top):
+    move = lambda k: top - k if top else k ^ 1
+    out = []
+    for z in range(NZ):
+        for yl in range(NYL):
+            for x in range(NX):
+                for yh in range(NYH):
+                    for c in range(NC):
+                        to = (move(z), yl, x) if axis == "z" else (z, yl, move(x))
+                        out.append((_flat(z, yl, x, yh, c), _flat(*to, yh, c)))
+    return out
+
+
+XE, XO, ZE, ZO = _pairs("x", 0), _pairs("x", 3), _pairs("z", 0), _pairs("z", 3)
 
 
 def send(value, pairs):
     return lax.ppermute(value, AXES, pairs)
+
+
+def tie(value, *deps):
+    return lax.optimization_barrier((value, *deps))[0]
 
 
 def _sorted(v):
@@ -125,7 +147,7 @@
         f = (word >> 8) & 31
         acc[r] += jnp.dot(tile[...], feats[f], preferred_element_type=F32)
 
-    prime, body = _tile_loop(tab, first, count, tiles, tbuf, tsem, step, 2)
+    prime, body = _tile_loop(tab, first, count, tiles, tbuf, tsem, step, UNROLL)
     prime()
     copies = []
     at = 0
@@ -201,7 +223,7 @@
         r = (word >> 8) & 7
         acc[f] += jnp.dot(dagg[r], tile[...], preferred_element_type=F32)
 
-    prime, body = _tile_loop(tab, first, count, tiles, tbuf, tsem, step, 2)
+    prime, body = _tile_loop(tab, first, count, tiles, tbuf, tsem, step, UNROLL)
     prime()
     copies = [
         pltpu.make_async_copy(d0, dagg.at[pl.ds(0, 4)], dsem.at[0]),
@@ -252,10 +274,10 @@
     )(tab, offs, tiles, d0, d1)
 
 
-def _dense_kernel(mine, core, far, cot0, cot1, w_ref, act, dagg, wterm):
+def _dense_kernel(near, far, cot0, cot1, w_ref, act, dagg, wterm):
     w = w_ref[...]
     for k in range(4):
-        agg = (mine[k] + core[k] + far[(k + 2) % 4].astype(F32)).astype(BF16)
+        agg = (near[k].astype(F32) + far[(k + 2) % 4].astype(F32)).astype(BF16)
         pre = jnp.dot(agg, w, preferred_element_type=F32)
         sig = jax.nn.sigmoid(pre)
         cot = (cot0 if k < 2 else cot1)[k % 2].astype(F32)
@@ -263,30 +285,31 @@
         dagg[k] = lax.dot_general(
             w, dpre, (((1,), (1,)), ((), ())), preferred_element_type=F32
         ).astype(BF16)
+        term = lax.dot_general(agg, dpre, (((0,), (0,)), ((), ())), preferred_element_type=F32)
         if k < 2:
             act[k] = (pre * sig).astype(BF16)
-            term = lax.dot_general(
-                agg, dpre, (((0,), (0,)), ((), ())), preferred_element_type=F32
-            )
-            wterm[...] = term if k == 0 else wterm[...] + term
-
-
-def dense(mine, core, far, cot0, cot1, w):
+        if k % 2 == 0:
+            wterm[k // 2] = term
+        else:
+            wterm[k // 2] = wterm[k // 2] + term
+
+
+def dense(near, far, cot0, cot1, w):
     return pl.pallas_call(
         _dense_kernel,
         name="dense",
-        in_specs=[VMEM] * 6,
+        in_specs=[VMEM] * 5,
         out_specs=[VMEM] * 3,
         out_shape=[
             jax.ShapeDtypeStruct((2, B, B), BF16),
             jax.ShapeDtypeStruct((4, B, B), BF16),
-            jax.ShapeDtypeStruct((B, B), F32),
+            jax.ShapeDtypeStruct((2, B, B), F32),
         ],
         compiler_params=pltpu.CompilerParams(vmem_limit_bytes=16 * MIB),
         cost_estimate=pl.CostEstimate(
             flops=10 * 2 * B**3, bytes_accessed=5 * MIB, transcendentals=1024 * 256
         ),
-    )(mine, core, far, cot0, cot1, w)
+    )(near, far, cot0, cot1, w)
 
 
 def plus(*terms):
@@ -296,72 +319,74 @@
     return total.astype(BF16)
 
 
-def gather(own):
-    other = send(own, YN)
-    e0 = jnp.stack([own[0], other[0]])
-    o0 = jnp.stack([own[1], other[1]])
-    e_m, e_p = send(e0, XP), send(e0, XM)
-    o_m, o_p = send(o0, ZP), send(o0, ZM)
-    e_a, e_b = send(e_m[:1], XP), send(e_p[1:], XM)
-    o_a, o_b = send(o_m[:1], ZP), send(o_p[1:], ZM)
-    even = jnp.concatenate([e0, e_m, e_p, e_a, e_b])
-    odd = jnp.concatenate([o0, o_m, o_p, o_a, o_b])
-    em, ep = send(even, ZP), send(even, ZM)
-    om, op = send(odd, XP), send(odd, XM)
-    ea, eb = send(em[:4], ZP), send(ep[4:], ZM)
-    oa, ob = send(om[:4], XP), send(op[4:], XM)
-    return [even, odd], [em, ep, om, op], [ea, eb, oa, ob]
+def weight_sum(term, c, yh):
+    a, b = term[0], term[1]
+    half = B // 2
+    whole = a + b
+    keep = lax.dynamic_slice_in_dim(whole, c * half, half, 0)
+    give = lax.dynamic_slice_in_dim(whole, (1 - c) * half, half, 0)
+    keep = keep + send(give, CC)
+    for pairs in (YN, XE, ZE, XO, ZO):
+        keep = keep + send(keep, pairs)
+    got = send(keep, CC)
+    return jnp.where(c == 0, jnp.concatenate([keep, got]), jnp.concatenate([got, keep]))
 
 
 def body(node_feats, weight, cotangent, tiles, tile_rows, tile_cols, tile_count):
     node, rep = lax.axis_index("node"), lax.axis_index("rep")
     x, yl, z = node % NX, node // NX % NYL, node // (NX * NYL)
     c, yh = rep % NC, rep // NC
-    tiles = tiles[0, 0]
+    tiles = pltpu.with_memory_space_constraint(tiles[0, 0], pltpu.HBM)
     fwd, bwd, offs = tables(
         tile_rows[0, 0], tile_cols[0, 0], tile_count[0, 0], z, yl, x, yh, c
     )
     own = lax.dynamic_slice_in_dim(node_feats.reshape(8, B, B), rep * 2, 2, 0)
     cot0 = cotangent.reshape(2, B, B)
-    cot1 = send(cot0, YH)
-    near, mid, far = gather(own)
-    acc = forward(0, fwd, offs, tiles, near, None, 0.25)
-    acc = forward(1, fwd, offs, tiles, mid, acc, 0.5)
-    mine, theirs = forward(2, fwd, offs, tiles, far, acc, 0.25)
+
+    other = send(own, YN)
+    e0 = jnp.stack([own[0], other[0]])
+    o0 = jnp.stack([own[1], other[1]])
+    e_m, e_p, e_2 = send(e0, XP), send(e0, XM), send(e0, X2)
+    o_m, o_p, o_2 = send(o0, ZP), send(o0, ZM), send(o0, Z2)
+    even = jnp.concatenate([e0, e_m, e_p, e_2])
+    odd = jnp.concatenate([o0, o_m, o_p, o_2])
+    cot1 = send(tie(cot0, even, odd), YH)
+    em, ep = send(even, ZP), send(even, ZM)
+    om, op = send(odd, XP), send(odd, XM)
+    acc = forward(0, fwd, offs, tiles, [even, odd], None, 0.25)
+    em, ep, om, op, acc, cot1 = lax.optimization_barrier((em, ep, om, op, acc, cot1))
+    ea, eb = send(em[:4], ZP), send(ep[4:], ZM)
+    oa, ob = send(om[:4], XP), send(op[4:], XM)
+    acc = forward(1, fwd, offs, tiles, [em, ep, om, op], acc, 0.5)
+    mine, theirs = forward(2, fwd, offs, tiles, [ea, eb, oa, ob], acc, 0.25)
     core = send(theirs, CC)
-    across = send((mine + core).astype(BF16), YH)
-    act, d0, term = dense(mine, core, across, cot0, cot1, weight)
+    part = (mine + core).astype(BF16)
+    across = send(part, YH)
+    act, d0, term = dense(part, across, cot0, cot1, weight)
     d1 = send(d0, CC)
-    scale = float(node_feats.shape[0] * NZ * NYL * NX) ** (-0.5)
-    weight_grad = lax.psum(term, AXES) * scale
 
     ea, eb, oa, ob = backward(2, bwd, offs, tiles, d0, d1, [4, 4, 4, 4], 0.25)
     ra, rb = send(ea, ZP), send(eb, ZM)
     sa, sb = send(oa, XP), send(ob, XM)
-    em0, em1, ep0, ep1, om0, om1, op0, op1 = backward(
-        1, bwd, offs, tiles, d0, d1, [4] * 8, 0.5
+    d0, d1, ea, eb, oa, ob = lax.optimization_barrier((d0, d1, ea, eb, oa, ob))
+    em, ep, om, op = backward(1, bwd, offs, tiles, d0, d1, [8] * 4, 0.5)
+    even, odd = backward(0, bwd, offs, tiles, d0, d1, [8, 8], 0.25)
+    em, ep, om, op, even, odd, ra, rb, sa, sb = lax.optimization_barrier(
+        (em, ep, om, op, even, odd, ra, rb, sa, sb)
     )
-    even, odd = backward(0, bwd, offs, tiles, d0, d1, [8, 8], 0.25)
-    to_zp = jnp.concatenate([plus(ep0, ra), ep1])
-    to_zm = jnp.concatenate([em0, plus(em1, rb)])
-    to_xp = jnp.concatenate([plus(op0, sa), op1])
-    to_xm = jnp.concatenate([om0, plus(om1, sb)])
-    even = plus(even, send(to_zp, ZP), send(to_zm, ZM))
-    odd = plus(odd, send(to_xp, XP), send(to_xm, XM))
-
-    def inner(q, up, down):
-        ca, cb = send(q[6:7], up), send(q[7:8], down)
-        to_up = jnp.concatenate([plus(q[4:5], ca), q[5:6]])
-        to_down = jnp.concatenate([q[2:3], plus(q[3:4], cb)])
-        return q[0:2], send(to_up, up), send(to_down, down)
-
-    ge = inner(even, XP, XM)
-    go = inner(odd, ZP, ZM)
-    ge = plus(*ge)
-    go = plus(*go)
+    ep = ep.at[:4].set(plus(ep[:4], ra))
+    em = em.at[4:].set(plus(em[4:], rb))
+    op = op.at[:4].set(plus(op[:4], sa))
+    om = om.at[4:].set(plus(om[4:], sb))
+    even = plus(even, send(ep, ZP), send(em, ZM))
+    odd = plus(odd, send(op, XP), send(om, XM))
+    ge = plus(even[0:2], send(even[4:6], XP), send(even[2:4], XM), send(even[6:8], X2))
+    go = plus(odd[0:2], send(odd[4:6], ZP), send(odd[2:4], ZM), send(odd[6:8], Z2))
     other = send(jnp.stack([ge[1], go[1]]), YN)
     total = jnp.stack([ge[0], go[0]]).astype(F32) + other.astype(F32)
     feature_grad = jnp.swapaxes(total, 1, 2).astype(BF16).reshape(2 * B, B)
+    scale = float(node_feats.shape[0] * NZ * NYL * NX) ** (-0.5)
+    weight_grad = weight_sum(term, c, yh) * scale
     return act.reshape(2 * B, B), feature_grad, weight_grad
 
 

time: 374 us -> 203 us (0.54)
  Pallas kernels: 94.8 us -> 43.2 us
  waiting for transfers between devices: 149 us -> 98.7 us
  local copies, waits for them, and re-layouts: 32.1 us -> 3.29 us
  starting transfers between devices: 69.4 us -> 51.6 us
  between operations: 15.2 us -> 1.83 us
  other arithmetic: 10.4 us -> 4.1 us
    psum x1 -> x0, waiting for transfers between devices: 94.3 us -> none  [body(): weight_grad = lax.psum(term, AXES) * scale]
    ppermute x38 -> x41, waiting for transfers between devices: 54.5 us -> 98.7 us  [send(): return lax.ppermute(value, AXES, pairs)]
    unnamed x21 -> x13, local copies, waits for them, and re-layouts: 26.9 us -> 1.1 us
    pallas_call x3, Pallas kernels: 48.6 us -> 22.9 us  [forward(): pl.pallas_call(functools.partial(_forward_kernel, chunk, len(bufs), last)...]
    pallas_call x3, Pallas kernels: 44.6 us -> 18.9 us  [backward(): pl.pallas_call(functools.partial(_backward_kernel, chunk, len(sizes)), na...]
    ppermute x38 -> x41, starting transfers between devices: 69.4 us -> 51.6 us  [send(): return lax.ppermute(value, AXES, pairs)]
  transfers between devices with their start and end apart: 39 -> 41, of which waited for: 15 -> 21; matrix products, arithmetic and copies ran while one was open for 5% -> 3% of each run, Pallas kernels for 19% -> 14%
where the time goes in v2:
time: 203 us
  waiting for transfers between devices  98.7 us (49%)
  starting transfers between devices  51.6 us (25%)
  Pallas kernels  43.2 us (21%)
  other arithmetic  4.1 us (2%)
  local copies, waits for them, and re-layouts  3.29 us (2%)
    ppermute x41, waiting for transfers between devices, send(): return lax.ppermute(value, AXES, pairs)  98.7 us
    ppermute x41, starting transfers between devices, send(): return lax.ppermute(value, AXES, pairs)  51.6 us
    pallas_call x3, Pallas kernels, forward(): pl.pallas_call(functools.partial(_forward_kernel, chunk, len(bufs), last)...  22.9 us
    pallas_call x3, Pallas kernels, backward(): pl.pallas_call(functools.partial(_backward_kernel, chunk, len(sizes)), na...  18.9 us
  transfers between devices with their start and end apart: 41, of which 21 were waited for; matrix products, arithmetic and copies ran while one was open for 3% of the time, Pallas kernels for 14%

profile of v2, /device:TPU:0, one launch (start us, length us, event | category | flops | bytes accessed | tf_op | source)
XLA Modules:
  0.0 202.7 jit_solution(14707665449869118588)
XLA Ops:
  0.6 1.0 constant_dynamic-slice_fusion.1
  1.6 1.7 collective-permute-start
  3.4 1.0 constant_dynamic-update-slice_fusion.9
  4.4 5.3 %collective-permute-done = bf16[2,256,256]{2,1,0:T(8,128)(2,1)S(1)} collective-permute-done((bf16[2,256,256]{2,1,0:T(8,128)(2,1)S(1)}, bf16[2,256,256]{2,1,0:T(8,128)(2,1)S(1)}, u32[]{:S(2)}, u32[]{:S(2)}) %collective-permute-start) | collective-permute-done | bytes 262176 | tf_op jit(solution)/shard_map/ppermute | solution.py:61
  9.8 2.1 %collective-permute-start.6 = (bf16[2,256,256]{2,1,0:T(8,128)(2,1)S(1)}, bf16[2,256,256]{2,1,0:T(8,128)(2,1)S(1)}, u32[]{:S(2)}, u32[]{:S(2)}) collective-permute-start(bf16[2,256,256]{2,1,0:T(8,128)(2,1)S(1)} %pad_maximum_fusion.1), channel_id=1, source_target_pairs={{0,32},{1,33},{2,34},{3,35},{4,36},{5,37},{6,38},{7,39},{8,40},{9,... | collective-permute-start | bytes 786440 | tf_op jit(solution)/shard_map/ppermute | solution.py:61
  11.9 2.2 %collective-permute-start.7 = (bf16[2,256,256]{2,1,0:T(8,128)(2,1)S(1)}, bf16[2,256,256]{2,1,0:T(8,128)(2,1)S(1)}, u32[]{:S(2)}, u32[]{:S(2)}) collective-permute-start(bf16[2,256,256]{2,1,0:T(8,128)(2,1)S(1)} %pad_maximum_fusion.1), channel_id=1, source_target_pairs={{0,96},{1,97},{2,98},{3,99},{4,100},{5,101},{6,102},{7,103},{8,104... | collective-permute-start | bytes 786440 | tf_op jit(solution)/shard_map/ppermute | solution.py:61
  14.8 1.9 collective-permute-start.8
  16.7 3.1 %collective-permute-start.3 = (bf16[2,256,256]{2,1,0:T(8,128)(2,1)S(1)}, bf16[2,256,256]{2,1,0:T(8,128)(2,1)S(1)}, u32[]{:S(2)}, u32[]{:S(2)}) collective-permute-start(bf16[2,256,256]{2,1,0:T(8,128)(2,1)S(1)} %pad_maximum_fusion), channel_id=1, source_target_pairs={{0,8},{1,9},{2,10},{3,11},{4,12},{5,13},{6,14},{7,15},{8,0},{9,1},... | collective-permute-start | bytes 786440 | tf_op jit(solution)/shard_map/ppermute | solution.py:61
  19.8 1.1 collective-permute-start.2
  20.9 0.9 collective-permute-start.1
  21.9 2.6 %collective-permute-done.7 = bf16[2,256,256]{2,1,0:T(8,128)(2,1)S(1)} collective-permute-done((bf16[2,256,256]{2,1,0:T(8,128)(2,1)S(1)}, bf16[2,256,256]{2,1,0:T(8,128)(2,1)S(1)}, u32[]{:S(2)}, u32[]{:S(2)}) %collective-permute-start.7) | collective-permute-done | bytes 262176 | tf_op jit(solution)/shard_map/ppermute | solution.py:61
  24.5 1.8 collective-permute-done.8
  26.3 2.8 %collective-permute-start.10 = (bf16[8,256,256]{2,1,0:T(8,128)(2,1)S(1)}, bf16[8,256,256]{2,1,0:T(8,128)(2,1)S(1)}, u32[]{:S(2)}, u32[]{:S(2)}) collective-permute-start(bf16[8,256,256]{2,1,0:T(8,128)(2,1)S(1)} %constant_dynamic-update-slice_fusion.5.refs_1_), channel_id=1, source_target_pairs={{0,12},{1,13},{2,14},{3,15},{4,0},{5,1},{6,2},{7,3},{8,4},{9,5},{1... | collective-permute-start | bytes 3145736 | tf_op jit(solution)/shard_map/ppermute | solution.py:61
  29.1 2.0 %collective-permute-done.1 = bf16[2,256,256]{2,1,0:T(8,128)(2,1)S(1)} collective-permute-done((bf16[2,256,256]{2,1,0:T(8,128)(2,1)S(1)}, bf16[2,256,256]{2,1,0:T(8,128)(2,1)S(1)}, u32[]{:S(2)}, u32[]{:S(2)}) %collective-permute-start.1) | collective-permute-done | bytes 262176 | tf_op jit(solution)/shard_map/ppermute | solution.py:61
  31.2 2.0 collective-permute-done.2
  34.1 1.3 collective-permute-start.4
  35.7 3.3 %collective-permute-start.11 = (bf16[2,256,256]{2,1,0:T(8,128)(2,1)S(1)}, bf16[2,256,256]{2,1,0:T(8,128)(2,1)S(1)}, u32[]{:S(2)}, u32[]{:S(2)}) collective-permute-start(bf16[2,256,256]{2,1,0:T(8,128)(2,1)S(1)} %bitcast.15), channel_id=1, source_target_pairs={{0,2},{1,3},{2,0},{3,1},{4,6},{5,7},{6,4},{7,5},{8,10},{9,11},{10,... | collective-permute-start | bytes 786440 | tf_op jit(solution)/shard_map/ppermute | solution.py:61
  39.2 5.6 %tiles_forward_0.1.refs_4_ = f32[8,256,256]{2,1,0:T(8,128)S(1)} custom-call(s32[160]{0:T(256)S(1)} %select_reduce_fusion.1.tab, s32[4]{0:T(128)S(1)} %convert_reduce_fusion.2.offs, bf16[160,256,256]{2,1,0:T(8,128)(2,1)} %bitcast.17, bf16[8,256,256]{2,1,0:T(8,128)(2,1)S(1)} %constant_dynamic-update-slice_fusion.refs_0_, ...), custom_call_target="tpu_custom_call" | custom-call | flops 1342177280 | bytes 11534336 | tf_op jit(solution)/shard_map/tiles_forward_0/pallas_call | solution.py:194
  44.8 8.0 %collective-permute-done.10.refs_3_ = bf16[8,256,256]{2,1,0:T(8,128)(2,1)S(1)} collective-permute-done((bf16[8,256,256]{2,1,0:T(8,128)(2,1)S(1)}, bf16[8,256,256]{2,1,0:T(8,128)(2,1)S(1)}, u32[]{:S(2)}, u32[]{:S(2)}) %collective-permute-start.10) | collective-permute-done | bytes 1048608 | tf_op jit(solution)/shard_map/ppermute | solution.py:61
  54.0 2.8 %collective-permute-done.4.refs_0_ = bf16[8,256,256]{2,1,0:T(8,128)(2,1)S(1)} collective-permute-done((bf16[8,256,256]{2,1,0:T(8,128)(2,1)S(1)}, bf16[8,256,256]{2,1,0:T(8,128)(2,1)S(1)}, u32[]{:S(2)}, u32[]{:S(2)}) %collective-permute-start.4) | collective-permute-done | bytes 1048608 | tf_op jit(solution)/shard_map/ppermute | solution.py:61
  57.0 3.2 %collective-permute-start.13 = (bf16[4,256,256]{2,1,0:T(8,128)(2,1)S(1)}, bf16[4,256,256]{2,1,0:T(8,128)(2,1)S(1)}, u32[]{:S(2)}, u32[]{:S(2)}) collective-permute-start(bf16[4,256,256]{2,1,0:T(8,128)(2,1)S(1)} %slice.171), channel_id=1, source_target_pairs={{0,96},{1,97},{2,98},{3,99},{4,100},{5,101},{6,102},{7,103},{8,104... | collective-permute-start | bytes 1572872 | tf_op jit(solution)/shard_map/ppermute | solution.py:61
  60.2 1.9 collective-permute-start.14
  62.1 1.4 collective-permute-start.15
  63.5 9.4 %tiles_forward_1.1.refs_4_ = f32[8,256,256]{2,1,0:T(8,128)S(1)} custom-call(s32[160]{0:T(256)S(1)} %select_reduce_fusion.1.tab, s32[4]{0:T(128)S(1)} %convert_reduce_fusion.2.offs, bf16[160,256,256]{2,1,0:T(8,128)(2,1)} %bitcast.18, bf16[8,256,256]{2,1,0:T(8,128)(2,1)S(1)} %collective-permute-done.4.refs_0_, ...), custom_call_target="tpu_custom_call" | custom-call | flops 2684354560 | bytes 16777216 | tf_op jit(solution)/shard_map/tiles_forward_1/pallas_call | solution.py:194
  72.9 7.9 %tiles_forward_2.1 = (f32[4,256,256]{2,1,0:T(8,128)S(1)}, f32[4,256,256]{2,1,0:T(8,128)S(1)}) custom-call(s32[160]{0:T(256)S(1)} %select_reduce_fusion.1.tab, s32[4]{0:T(128)S(1)} %convert_reduce_fusion.2.offs, bf16[160,256,256]{2,1,0:T(8,128)(2,1)} %bitcast.19, bf16[4,256,256]{2,1,0:T(8,128)(2,1)S(1)} %collective-permute-done.12.refs_0_, ...), custom_call_target="tpu_custom_call" | custom-call | flops 1342177280 | bytes 11534336 | tf_op jit(solution)/shard_map/tiles_forward_2/pallas_call | solution.py:194
  80.9 2.6 %collective-permute-done.16 = f32[4,256,256]{2,1,0:T(8,128)S(1)} collective-permute-done((f32[4,256,256]{2,1,0:T(8,128)S(1)}, f32[4,256,256]{2,1,0:T(8,128)S(1)}, u32[]{:S(2)}, u32[]{:S(2)}) %collective-permute-start.16) | collective-permute-done | bytes 1048608 | tf_op jit(solution)/shard_map/ppermute | solution.py:61
  83.9 15.5 %collective-permute-done.17.far = bf16[4,256,256]{2,1,0:T(8,128)(2,1)S(1)} collective-permute-done((bf16[4,256,256]{2,1,0:T(8,128)(2,1)S(1)}, bf16[4,256,256]{2,1,0:T(8,128)(2,1)S(1)}, u32[]{:S(2)}, u32[]{:S(2)}) %collective-permute-start.17) | collective-permute-done | bytes 524320 | tf_op jit(solution)/shard_map/ppermute | solution.py:61
  99.3 1.4 dense.1
  101.1 1.6 collective-permute-done.18.d1
  102.6 6.4 %tiles_backward_2.1 = (bf16[4,256,256]{2,1,0:T(8,128)(2,1)S(1)}, bf16[4,256,256]{2,1,0:T(8,128)(2,1)S(1)}, bf16[4,256,256]{2,1,0:T(8,128)(2,1)S(1)}, bf16[4,256,256]{2,1,0:T(8,128)(2,1)S(1)}) custom-call(s32[160]{0:T(256)S(1)} %select_reduce_fusion.tab, s32[4]{0:T(128)S(1)} %convert_reduce_fusion.2.offs, bf16[160,256,256]{2,1,0:T(8,128)(2,1)} %bitcast.20, ...), custom_call_target="tpu_custom_call" | custom-call | flops 1342177280 | bytes 11534336 | tf_op jit(solution)/shard_map/tiles_backward_2/pallas_call | solution.py:255
  109.2 3.2 %collective-permute-start.20 = (bf16[4,256,256]{2,1,0:T(8,128)(2,1)S(1)}, bf16[4,256,256]{2,1,0:T(8,128)(2,1)S(1)}, u32[]{:S(2)}, u32[]{:S(2)}) collective-permute-start(bf16[4,256,256]{2,1,0:T(8,128)(2,1)S(1)} %get-tuple-element.97), channel_id=1, source_target_pairs={{0,96},{1,97},{2,98},{3,99},{4,100},{5,101},{6,102},{7,103},{8,104... | collective-permute-start | bytes 1572872 | tf_op jit(solution)/shard_map/ppermute | solution.py:61
  112.4 1.3 collective-permute-start.21
  113.7 2.0 collective-permute-start.22
  115.8 4.8 %tiles_backward_0.1 = (bf16[8,256,256]{2,1,0:T(8,128)(2,1)S(1)}, bf16[8,256,256]{2,1,0:T(8,128)(2,1)S(1)}) custom-call(s32[160]{0:T(256)S(1)} %select_reduce_fusion.tab, s32[4]{0:T(128)S(1)} %convert_reduce_fusion.2.offs, bf16[160,256,256]{2,1,0:T(8,128)(2,1)} %bitcast.21, bf16[4,256,256]{2,1,0:T(8,128)(2,1)S(1)} %get-tuple-element.100.d0, ...), custom_call_target="tpu_custom_call" | custom-call | flops 1342177280 | bytes 11534336 | tf_op jit(solution)/shard_map/tiles_backward_0/pallas_call | solution.py:255
  120.6 7.6 %tiles_backward_1.1 = (bf16[8,256,256]{2,1,0:T(8,128)(2,1)S(1)}, bf16[8,256,256]{2,1,0:T(8,128)(2,1)S(1)}, bf16[8,256,256]{2,1,0:T(8,128)(2,1)S(1)}, bf16[8,256,256]{2,1,0:T(8,128)(2,1)S(1)}) custom-call(s32[160]{0:T(256)S(1)} %select_reduce_fusion.tab, s32[4]{0:T(128)S(1)} %convert_reduce_fusion.2.offs, bf16[160,256,256]{2,1,0:T(8,128)(2,1)} %bitcast.22, ...), custom_call_target="tpu_custom_call" | custom-call | flops 2684354560 | bytes 16777216 | tf_op jit(solution)/shard_map/tiles_backward_1/pallas_call | solution.py:255
  129.5 1.5 collective-permute-start.28
  131.0 3.3 %collective-permute-start.35 = (f32[128,256]{1,0:T(8,128)S(1)}, f32[128,256]{1,0:T(8,128)S(1)}, u32[]{:S(2)}, u32[]{:S(2)}) collective-permute-start(f32[128,256]{1,0:T(8,128)S(1)} %bitcast_add_fusion), channel_id=1, source_target_pairs={{0,16},{1,17},{2,18},{3,19},{4,20},{5,21},{6,22},{7,23},{8,24},{9,... | collective-permute-start | bytes 393224 | tf_op jit(solution)/shard_map/ppermute | solution.py:61
  134.8 2.1 %collective-permute-start.23 = (bf16[8,256,256]{2,1,0:T(8,128)(2,1)S(1)}, bf16[8,256,256]{2,1,0:T(8,128)(2,1)S(1)}, u32[]{:S(2)}, u32[]{:S(2)}) collective-permute-start(bf16[8,256,256]{2,1,0:T(8,128)(2,1)S(1)} %fusion), channel_id=1, source_target_pairs={{0,32},{1,33},{2,34},{3,35},{4,36},{5,37},{6,38},{7,39},{8,40},{9,... | collective-permute-start | bytes 3145736 | tf_op jit(solution)/shard_map/ppermute | solution.py:61
  137.9 19.0 %collective-permute-done.36 = f32[128,256]{1,0:T(8,128)S(1)} collective-permute-done((f32[128,256]{1,0:T(8,128)S(1)}, f32[128,256]{1,0:T(8,128)S(1)}, u32[]{:S(2)}, u32[]{:S(2)}) %collective-permute-start.36) | collective-permute-done | bytes 131104 | tf_op jit(solution)/shard_map/ppermute | solution.py:61
  157.1 6.0 %collective-permute-done.37 = f32[128,256]{1,0:T(8,128)S(1)} collective-permute-done((f32[128,256]{1,0:T(8,128)S(1)}, f32[128,256]{1,0:T(8,128)S(1)}, u32[]{:S(2)}, u32[]{:S(2)}) %collective-permute-start.37) | collective-permute-done | bytes 131104 | tf_op jit(solution)/shard_map/ppermute | solution.py:61
  163.2 6.4 %collective-permute-done.38 = f32[128,256]{1,0:T(8,128)S(1)} collective-permute-done((f32[128,256]{1,0:T(8,128)S(1)}, f32[128,256]{1,0:T(8,128)S(1)}, u32[]{:S(2)}, u32[]{:S(2)}) %collective-permute-start.38) | collective-permute-done | bytes 131104 | tf_op jit(solution)/shard_map/ppermute | solution.py:61
  170.8 4.2 %collective-permute-start.32 = (bf16[2,256,256]{2,1,0:T(8,128)(2,1)S(1)}, bf16[2,256,256]{2,1,0:T(8,128)(2,1)S(1)}, u32[]{:S(2)}, u32[]{:S(2)}) collective-permute-start(bf16[2,256,256]{2,1,0:T(8,128)(2,1)S(1)} %get-tuple-element.131), channel_id=1, source_target_pairs={{0,64},{1,65},{2,66},{3,67},{4,68},{5,69},{6,70},{7,71},{8,72},{9,... | collective-permute-start | bytes 786440 | tf_op jit(solution)/shard_map/ppermute | solution.py:61
  176.5 10.0 %collective-permute-done.30 = bf16[2,256,256]{2,1,0:T(8,128)(2,1)S(1)} collective-permute-done((bf16[2,256,256]{2,1,0:T(8,128)(2,1)S(1)}, bf16[2,256,256]{2,1,0:T(8,128)(2,1)S(1)}, u32[]{:S(2)}, u32[]{:S(2)}) %collective-permute-start.30) | collective-permute-done | bytes 262176 | tf_op jit(solution)/shard_map/ppermute | solution.py:61
  186.6 2.3 %collective-permute-start.26 = (bf16[2,256,256]{2,1,0:T(8,128)(2,1)S(1)}, bf16[2,256,256]{2,1,0:T(8,128)(2,1)S(1)}, u32[]{:S(2)}, u32[]{:S(2)}) collective-permute-start(bf16[2,256,256]{2,1,0:T(8,128)(2,1)S(1)} %get-tuple-element.129), channel_id=1, source_target_pairs={{0,12},{1,13},{2,14},{3,15},{4,0},{5,1},{6,2},{7,3},{8,4},{9,5},{1... | collective-permute-start | bytes 786440 | tf_op jit(solution)/shard_map/ppermute | solution.py:61
  189.1 5.2 %collective-permute-done.27 = bf16[2,256,256]{2,1,0:T(8,128)(2,1)S(1)} collective-permute-done((bf16[2,256,256]{2,1,0:T(8,128)(2,1)S(1)}, bf16[2,256,256]{2,1,0:T(8,128)(2,1)S(1)}, u32[]{:S(2)}, u32[]{:S(2)}) %collective-permute-start.27) | collective-permute-done | bytes 262176 | tf_op jit(solution)/shard_map/ppermute | solution.py:61
  195.9 1.3 collective-permute-done.40
  197.9 3.9 %collective-permute-done.33 = bf16[2,256,256]{2,1,0:T(8,128)(2,1)S(1)} collective-permute-done((bf16[2,256,256]{2,1,0:T(8,128)(2,1)S(1)}, bf16[2,256,256]{2,1,0:T(8,128)(2,1)S(1)}, u32[]{:S(2)}, u32[]{:S(2)}) %collective-permute-start.33) | collective-permute-done | bytes 262176 | tf_op jit(solution)/shard_map/ppermute | solution.py:61
  201.8 0.8 copy.11
  (97 shorter events, 12.0 us)
Async XLA Ops:
  1.6 8.0 %collective-permute-start = (bf16[2,256,256]{2,1,0:T(8,128)(2,1)S(1)}, bf16[2,256,256]{2,1,0:T(8,128)(2,1)S(1)}, u32[]{:S(2)}, u32[]{:S(2)}) collective-permute-start(bf16[2,256,256]{2,1,0:T(8,128)(2,1)S(1)} %constant_dynamic-slice_fusion.1), channel_id=1, source_target_pairs={{0,16},{1,17},{2,18},{3,19},{4,20},{5,21},{6,22},{7,23},{8,24},{9,... | collective-permute-start | bytes 786440 | tf_op jit(solution)/shard_map/ppermute | solution.py:61
  9.7 25.7 %copy-start.2 = (s32[1,1,160]{2,1,0:T(1,128)S(1)}, s32[1,1,160]{2,1,0:T(1,128)}, u32[]{:S(2)}) copy-start(s32[1,1,160]{2,1,0:T(1,128)} %param.20) | copy-start | bytes 1924
  9.7 25.7 %copy-start.3 = (s32[1,1,160]{2,1,0:T(1,128)S(1)}, s32[1,1,160]{2,1,0:T(1,128)}, u32[]{:S(2)}) copy-start(s32[1,1,160]{2,1,0:T(1,128)} %param.19) | copy-start | bytes 1924
  9.7 25.9 %copy-start = (bf16[512,256]{1,0:T(8,128)(2,1)S(1)}, bf16[512,256]{1,0:T(8,128)(2,1)}, u32[]{:S(2)}) copy-start(bf16[512,256]{1,0:T(8,128)(2,1)} %param.17) | copy-start | bytes 786436
  9.8 11.2 %collective-permute-start.6 = (bf16[2,256,256]{2,1,0:T(8,128)(2,1)S(1)}, bf16[2,256,256]{2,1,0:T(8,128)(2,1)S(1)}, u32[]{:S(2)}, u32[]{:S(2)}) collective-permute-start(bf16[2,256,256]{2,1,0:T(8,128)(2,1)S(1)} %pad_maximum_fusion.1), channel_id=1, source_target_pairs={{0,32},{1,33},{2,34},{3,35},{4,36},{5,37},{6,38},{7,39},{8,40},{9,... | collective-permute-start | bytes 786440 | tf_op jit(solution)/shard_map/ppermute | solution.py:61
  11.9 12.5 %collective-permute-start.7 = (bf16[2,256,256]{2,1,0:T(8,128)(2,1)S(1)}, bf16[2,256,256]{2,1,0:T(8,128)(2,1)S(1)}, u32[]{:S(2)}, u32[]{:S(2)}) collective-permute-start(bf16[2,256,256]{2,1,0:T(8,128)(2,1)S(1)} %pad_maximum_fusion.1), channel_id=1, source_target_pairs={{0,96},{1,97},{2,98},{3,99},{4,100},{5,101},{6,102},{7,103},{8,104... | collective-permute-start | bytes 786440 | tf_op jit(solution)/shard_map/ppermute | solution.py:61
  14.8 11.5 %collective-permute-start.8 = (bf16[2,256,256]{2,1,0:T(8,128)(2,1)S(1)}, bf16[2,256,256]{2,1,0:T(8,128)(2,1)S(1)}, u32[]{:S(2)}, u32[]{:S(2)}) collective-permute-start(bf16[2,256,256]{2,1,0:T(8,128)(2,1)S(1)} %pad_maximum_fusion.1), channel_id=1, source_target_pairs={{0,64},{1,65},{2,66},{3,67},{4,68},{5,69},{6,70},{7,71},{8,72},{9,... | collective-permute-start | bytes 786440 | tf_op jit(solution)/shard_map/ppermute | solution.py:61
  16.7 16.6 %collective-permute-start.3 = (bf16[2,256,256]{2,1,0:T(8,128)(2,1)S(1)}, bf16[2,256,256]{2,1,0:T(8,128)(2,1)S(1)}, u32[]{:S(2)}, u32[]{:S(2)}) collective-permute-start(bf16[2,256,256]{2,1,0:T(8,128)(2,1)S(1)} %pad_maximum_fusion), channel_id=1, source_target_pairs={{0,8},{1,9},{2,10},{3,11},{4,12},{5,13},{6,14},{7,15},{8,0},{9,1},... | collective-permute-start | bytes 786440 | tf_op jit(solution)/shard_map/ppermute | solution.py:61
  19.8 13.4 %collective-permute-start.2 = (bf16[2,256,256]{2,1,0:T(8,128)(2,1)S(1)}, bf16[2,256,256]{2,1,0:T(8,128)(2,1)S(1)}, u32[]{:S(2)}, u32[]{:S(2)}) collective-permute-start(bf16[2,256,256]{2,1,0:T(8,128)(2,1)S(1)} %pad_maximum_fusion), channel_id=1, source_target_pairs={{0,12},{1,13},{2,14},{3,15},{4,0},{5,1},{6,2},{7,3},{8,4},{9,5},{1... | collective-permute-start | bytes 786440 | tf_op jit(solution)/shard_map/ppermute | solution.py:61
  20.9 10.2 %collective-permute-start.1 = (bf16[2,256,256]{2,1,0:T(8,128)(2,1)S(1)}, bf16[2,256,256]{2,1,0:T(8,128)(2,1)S(1)}, u32[]{:S(2)}, u32[]{:S(2)}) collective-permute-start(bf16[2,256,256]{2,1,0:T(8,128)(2,1)S(1)} %pad_maximum_fusion), channel_id=1, source_target_pairs={{0,4},{1,5},{2,6},{3,7},{4,8},{5,9},{6,10},{7,11},{8,12},{9,13},{1... | collective-permute-start | bytes 786440 | tf_op jit(solution)/shard_map/ppermute | solution.py:61
  26.3 26.5 %collective-permute-start.10 = (bf16[8,256,256]{2,1,0:T(8,128)(2,1)S(1)}, bf16[8,256,256]{2,1,0:T(8,128)(2,1)S(1)}, u32[]{:S(2)}, u32[]{:S(2)}) collective-permute-start(bf16[8,256,256]{2,1,0:T(8,128)(2,1)S(1)} %constant_dynamic-update-slice_fusion.5.refs_1_), channel_id=1, source_target_pairs={{0,12},{1,13},{2,14},{3,15},{4,0},{5,1},{6,2},{7,3},{8,4},{9,5},{1... | collective-permute-start | bytes 3145736 | tf_op jit(solution)/shard_map/ppermute | solution.py:61
  29.1 24.0 %collective-permute-start.9 = (bf16[8,256,256]{2,1,0:T(8,128)(2,1)S(1)}, bf16[8,256,256]{2,1,0:T(8,128)(2,1)S(1)}, u32[]{:S(2)}, u32[]{:S(2)}) collective-permute-start(bf16[8,256,256]{2,1,0:T(8,128)(2,1)S(1)} %constant_dynamic-update-slice_fusion.5.refs_1_), channel_id=1, source_target_pairs={{0,4},{1,5},{2,6},{3,7},{4,8},{5,9},{6,10},{7,11},{8,12},{9,13},{1... | collective-permute-start | bytes 3145736 | tf_op jit(solution)/shard_map/ppermute | solution.py:61
  33.3 20.7 %collective-permute-start.5 = (bf16[8,256,256]{2,1,0:T(8,128)(2,1)S(1)}, bf16[8,256,256]{2,1,0:T(8,128)(2,1)S(1)}, u32[]{:S(2)}, u32[]{:S(2)}) collective-permute-start(bf16[8,256,256]{2,1,0:T(8,128)(2,1)S(1)} %constant_dynamic-update-slice_fusion.refs_0_), channel_id=1, source_target_pairs={{0,96},{1,97},{2,98},{3,99},{4,100},{5,101},{6,102},{7,103},{8,104... | collective-permute-start | bytes 3145736 | tf_op jit(solution)/shard_map/ppermute | solution.py:61
  34.1 22.7 %collective-permute-start.4 = (bf16[8,256,256]{2,1,0:T(8,128)(2,1)S(1)}, bf16[8,256,256]{2,1,0:T(8,128)(2,1)S(1)}, u32[]{:S(2)}, u32[]{:S(2)}) collective-permute-start(bf16[8,256,256]{2,1,0:T(8,128)(2,1)S(1)} %constant_dynamic-update-slice_fusion.refs_0_), channel_id=1, source_target_pairs={{0,32},{1,33},{2,34},{3,35},{4,36},{5,37},{6,38},{7,39},{8,40},{9,... | collective-permute-start | bytes 3145736 | tf_op jit(solution)/shard_map/ppermute | solution.py:61
  35.7 9.1 %collective-permute-start.11 = (bf16[2,256,256]{2,1,0:T(8,128)(2,1)S(1)}, bf16[2,256,256]{2,1,0:T(8,128)(2,1)S(1)}, u32[]{:S(2)}, u32[]{:S(2)}) collective-permute-start(bf16[2,256,256]{2,1,0:T(8,128)(2,1)S(1)} %bitcast.15), channel_id=1, source_target_pairs={{0,2},{1,3},{2,0},{3,1},{4,6},{5,7},{6,4},{7,5},{8,10},{9,11},{10,... | collective-permute-start | bytes 786440 | tf_op jit(solution)/shard_map/ppermute | solution.py:61
  56.9 16.0 %collective-permute-start.12 = (bf16[4,256,256]{2,1,0:T(8,128)(2,1)S(1)}, bf16[4,256,256]{2,1,0:T(8,128)(2,1)S(1)}, u32[]{:S(2)}, u32[]{:S(2)}) collective-permute-start(bf16[4,256,256]{2,1,0:T(8,128)(2,1)S(1)} %slice.170), channel_id=1, source_target_pairs={{0,32},{1,33},{2,34},{3,35},{4,36},{5,37},{6,38},{7,39},{8,40},{9,... | collective-permute-start | bytes 1572872 | tf_op jit(solution)/shard_map/ppermute | solution.py:61
  57.0 15.9 %collective-permute-start.13 = (bf16[4,256,256]{2,1,0:T(8,128)(2,1)S(1)}, bf16[4,256,256]{2,1,0:T(8,128)(2,1)S(1)}, u32[]{:S(2)}, u32[]{:S(2)}) collective-permute-start(bf16[4,256,256]{2,1,0:T(8,128)(2,1)S(1)} %slice.171), channel_id=1, source_target_pairs={{0,96},{1,97},{2,98},{3,99},{4,100},{5,101},{6,102},{7,103},{8,104... | collective-permute-start | bytes 1572872 | tf_op jit(solution)/shard_map/ppermute | solution.py:61
  60.2 12.7 %collective-permute-start.14 = (bf16[4,256,256]{2,1,0:T(8,128)(2,1)S(1)}, bf16[4,256,256]{2,1,0:T(8,128)(2,1)S(1)}, u32[]{:S(2)}, u32[]{:S(2)}) collective-permute-start(bf16[4,256,256]{2,1,0:T(8,128)(2,1)S(1)} %slice.172), channel_id=1, source_target_pairs={{0,4},{1,5},{2,6},{3,7},{4,8},{5,9},{6,10},{7,11},{8,12},{9,13},{1... | collective-permute-start | bytes 1572872 | tf_op jit(solution)/shard_map/ppermute | solution.py:61
  62.1 10.8 %collective-permute-start.15 = (bf16[4,256,256]{2,1,0:T(8,128)(2,1)S(1)}, bf16[4,256,256]{2,1,0:T(8,128)(2,1)S(1)}, u32[]{:S(2)}, u32[]{:S(2)}) collective-permute-start(bf16[4,256,256]{2,1,0:T(8,128)(2,1)S(1)} %slice.173), channel_id=1, source_target_pairs={{0,12},{1,13},{2,14},{3,15},{4,0},{5,1},{6,2},{7,3},{8,4},{9,5},{1... | collective-permute-start | bytes 1572872 | tf_op jit(solution)/shard_map/ppermute | solution.py:61
  80.8 18.5 %copy-start.1 = (bf16[256,256]{1,0:T(8,128)(2,1)S(1)}, bf16[256,256]{1,0:T(8,128)(2,1)}, u32[]{:S(2)}) copy-start(bf16[256,256]{1,0:T(8,128)(2,1)} %w_ref.1) | copy-start | bytes 393220
  80.9 2.7 %collective-permute-start.16 = (f32[4,256,256]{2,1,0:T(8,128)S(1)}, f32[4,256,256]{2,1,0:T(8,128)S(1)}, u32[]{:S(2)}, u32[]{:S(2)}) collective-permute-start(f32[4,256,256]{2,1,0:T(8,128)S(1)} %get-tuple-element.92), channel_id=1, source_target_pairs={{0,1},{1,0},{2,3},{3,2},{4,5},{5,4},{6,7},{7,6},{8,9},{9,8},{10,11... | collective-permute-start | bytes 3145736 | tf_op jit(solution)/shard_map/ppermute | solution.py:61
  83.8 15.5 %collective-permute-start.17 = (bf16[4,256,256]{2,1,0:T(8,128)(2,1)S(1)}, bf16[4,256,256]{2,1,0:T(8,128)(2,1)S(1)}, u32[]{:S(2)}, u32[]{:S(2)}) collective-permute-start(bf16[4,256,256]{2,1,0:T(8,128)(2,1)S(1)} %add_convert_fusion.6.near), channel_id=1, source_target_pairs={{0,2},{1,3},{2,0},{3,1},{4,6},{5,7},{6,4},{7,5},{8,10},{9,11},{10,... | collective-permute-start | bytes 1572872 | tf_op jit(solution)/shard_map/ppermute | solution.py:61
  100.7 1.9 collective-permute-start.18
  109.1 19.2 %collective-permute-start.19 = (bf16[4,256,256]{2,1,0:T(8,128)(2,1)S(1)}, bf16[4,256,256]{2,1,0:T(8,128)(2,1)S(1)}, u32[]{:S(2)}, u32[]{:S(2)}) collective-permute-start(bf16[4,256,256]{2,1,0:T(8,128)(2,1)S(1)} %get-tuple-element.96), channel_id=1, source_target_pairs={{0,32},{1,33},{2,34},{3,35},{4,36},{5,37},{6,38},{7,39},{8,40},{9,... | collective-permute-start | bytes 1572872 | tf_op jit(solution)/shard_map/ppermute | solution.py:61
  109.2 19.1 %collective-permute-start.20 = (bf16[4,256,256]{2,1,0:T(8,128)(2,1)S(1)}, bf16[4,256,256]{2,1,0:T(8,128)(2,1)S(1)}, u32[]{:S(2)}, u32[]{:S(2)}) collective-permute-start(bf16[4,256,256]{2,1,0:T(8,128)(2,1)S(1)} %get-tuple-element.97), channel_id=1, source_target_pairs={{0,96},{1,97},{2,98},{3,99},{4,100},{5,101},{6,102},{7,103},{8,104... | collective-permute-start | bytes 1572872 | tf_op jit(solution)/shard_map/ppermute | solution.py:61
  112.4 15.9 %collective-permute-start.21 = (bf16[4,256,256]{2,1,0:T(8,128)(2,1)S(1)}, bf16[4,256,256]{2,1,0:T(8,128)(2,1)S(1)}, u32[]{:S(2)}, u32[]{:S(2)}) collective-permute-start(bf16[4,256,256]{2,1,0:T(8,128)(2,1)S(1)} %get-tuple-element.98), channel_id=1, source_target_pairs={{0,4},{1,5},{2,6},{3,7},{4,8},{5,9},{6,10},{7,11},{8,12},{9,13},{1... | collective-permute-start | bytes 1572872 | tf_op jit(solution)/shard_map/ppermute | solution.py:61
  113.7 14.6 %collective-permute-start.22 = (bf16[4,256,256]{2,1,0:T(8,128)(2,1)S(1)}, bf16[4,256,256]{2,1,0:T(8,128)(2,1)S(1)}, u32[]{:S(2)}, u32[]{:S(2)}) collective-permute-start(bf16[4,256,256]{2,1,0:T(8,128)(2,1)S(1)} %get-tuple-element.99), channel_id=1, source_target_pairs={{0,12},{1,13},{2,14},{3,15},{4,0},{5,1},{6,2},{7,3},{8,4},{9,5},{1... | collective-permute-start | bytes 1572872 | tf_op jit(solution)/shard_map/ppermute | solution.py:61
  115.7 15.2 %collective-permute-start.34 = (f32[128,256]{1,0:T(8,128)S(1)}, f32[128,256]{1,0:T(8,128)S(1)}, u32[]{:S(2)}, u32[]{:S(2)}) collective-permute-start(f32[128,256]{1,0:T(8,128)S(1)} %dynamic-slice_bitcast_fusion), channel_id=1, source_target_pairs={{0,1},{1,0},{2,3},{3,2},{4,5},{5,4},{6,7},{7,6},{8,9},{9,8},{10,11... | collective-permute-start | bytes 393224 | tf_op jit(solution)/shard_map/ppermute | solution.py:61
  128.5 41.2 %collective-permute-start.29 = (bf16[8,256,256]{2,1,0:T(8,128)(2,1)S(1)}, bf16[8,256,256]{2,1,0:T(8,128)(2,1)S(1)}, u32[]{:S(2)}, u32[]{:S(2)}) collective-permute-start(bf16[8,256,256]{2,1,0:T(8,128)(2,1)S(1)} %fusion.3), channel_id=1, source_target_pairs={{0,12},{1,13},{2,14},{3,15},{4,0},{5,1},{6,2},{7,3},{8,4},{9,5},{1... | collective-permute-start | bytes 3145736 | tf_op jit(solution)/shard_map/ppermute | solution.py:61
  129.5 40.3 %collective-permute-start.28 = (bf16[8,256,256]{2,1,0:T(8,128)(2,1)S(1)}, bf16[8,256,256]{2,1,0:T(8,128)(2,1)S(1)}, u32[]{:S(2)}, u32[]{:S(2)}) collective-permute-start(bf16[8,256,256]{2,1,0:T(8,128)(2,1)S(1)} %fusion.2), channel_id=1, source_target_pairs={{0,4},{1,5},{2,6},{3,7},{4,8},{5,9},{6,10},{7,11},{8,12},{9,13},{1... | collective-permute-start | bytes 3145736 | tf_op jit(solution)/shard_map/ppermute | solution.py:61
  131.0 6.6 %collective-permute-start.35 = (f32[128,256]{1,0:T(8,128)S(1)}, f32[128,256]{1,0:T(8,128)S(1)}, u32[]{:S(2)}, u32[]{:S(2)}) collective-permute-start(f32[128,256]{1,0:T(8,128)S(1)} %bitcast_add_fusion), channel_id=1, source_target_pairs={{0,16},{1,17},{2,18},{3,19},{4,20},{5,21},{6,22},{7,23},{8,24},{9,... | collective-permute-start | bytes 393224 | tf_op jit(solution)/shard_map/ppermute | solution.py:61
  134.5 40.5 %collective-permute-start.24 = (bf16[8,256,256]{2,1,0:T(8,128)(2,1)S(1)}, bf16[8,256,256]{2,1,0:T(8,128)(2,1)S(1)}, u32[]{:S(2)}, u32[]{:S(2)}) collective-permute-start(bf16[8,256,256]{2,1,0:T(8,128)(2,1)S(1)} %fusion.1), channel_id=1, source_target_pairs={{0,96},{1,97},{2,98},{3,99},{4,100},{5,101},{6,102},{7,103},{8,104... | collective-permute-start | bytes 3145736 | tf_op jit(solution)/shard_map/ppermute | solution.py:61
  134.8 40.7 %collective-permute-start.23 = (bf16[8,256,256]{2,1,0:T(8,128)(2,1)S(1)}, bf16[8,256,256]{2,1,0:T(8,128)(2,1)S(1)}, u32[]{:S(2)}, u32[]{:S(2)}) collective-permute-start(bf16[8,256,256]{2,1,0:T(8,128)(2,1)S(1)} %fusion), channel_id=1, source_target_pairs={{0,32},{1,33},{2,34},{3,35},{4,36},{5,37},{6,38},{7,39},{8,40},{9,... | collective-permute-start | bytes 3145736 | tf_op jit(solution)/shard_map/ppermute | solution.py:61
  137.6 19.4 %collective-permute-start.36 = (f32[128,256]{1,0:T(8,128)S(1)}, f32[128,256]{1,0:T(8,128)S(1)}, u32[]{:S(2)}, u32[]{:S(2)}) collective-permute-start(f32[128,256]{1,0:T(8,128)S(1)} %add.460), channel_id=1, source_target_pairs={{0,4},{1,5},{2,6},{3,7},{4,0},{5,1},{6,2},{7,3},{8,12},{9,13},{10,... | collective-permute-start | bytes 393224 | tf_op jit(solution)/shard_map/ppermute | solution.py:61
  157.0 6.1 %collective-permute-start.37 = (f32[128,256]{1,0:T(8,128)S(1)}, f32[128,256]{1,0:T(8,128)S(1)}, u32[]{:S(2)}, u32[]{:S(2)}) collective-permute-start(f32[128,256]{1,0:T(8,128)S(1)} %add.461), channel_id=1, source_target_pairs={{0,32},{1,33},{2,34},{3,35},{4,36},{5,37},{6,38},{7,39},{8,40},{9,... | collective-permute-start | bytes 393224 | tf_op jit(solution)/shard_map/ppermute | solution.py:61
  163.1 6.5 %collective-permute-start.38 = (f32[128,256]{1,0:T(8,128)S(1)}, f32[128,256]{1,0:T(8,128)S(1)}, u32[]{:S(2)}, u32[]{:S(2)}) collective-permute-start(f32[128,256]{1,0:T(8,128)S(1)} %add.462), channel_id=1, source_target_pairs={{0,12},{1,13},{2,14},{3,15},{4,8},{5,9},{6,10},{7,11},{8,4},{9,5},... | collective-permute-start | bytes 393224 | tf_op jit(solution)/shard_map/ppermute | solution.py:61
  169.6 26.1 %collective-permute-start.39 = (f32[128,256]{1,0:T(8,128)S(1)}, f32[128,256]{1,0:T(8,128)S(1)}, u32[]{:S(2)}, u32[]{:S(2)}) collective-permute-start(f32[128,256]{1,0:T(8,128)S(1)} %add.463), channel_id=1, source_target_pairs={{0,96},{1,97},{2,98},{3,99},{4,100},{5,101},{6,102},{7,103},{8,104... | collective-permute-start | bytes 393224 | tf_op jit(solution)/shard_map/ppermute | solution.py:61
  170.3 16.2 %collective-permute-start.30 = (bf16[2,256,256]{2,1,0:T(8,128)(2,1)S(1)}, bf16[2,256,256]{2,1,0:T(8,128)(2,1)S(1)}, u32[]{:S(2)}, u32[]{:S(2)}) collective-permute-start(bf16[2,256,256]{2,1,0:T(8,128)(2,1)S(1)} %get-tuple-element.130), channel_id=1, source_target_pairs={{0,32},{1,33},{2,34},{3,35},{4,36},{5,37},{6,38},{7,39},{8,40},{9,... | collective-permute-start | bytes 786440 | tf_op jit(solution)/shard_map/ppermute | solution.py:61
  170.8 15.8 %collective-permute-start.32 = (bf16[2,256,256]{2,1,0:T(8,128)(2,1)S(1)}, bf16[2,256,256]{2,1,0:T(8,128)(2,1)S(1)}, u32[]{:S(2)}, u32[]{:S(2)}) collective-permute-start(bf16[2,256,256]{2,1,0:T(8,128)(2,1)S(1)} %get-tuple-element.131), channel_id=1, source_target_pairs={{0,64},{1,65},{2,66},{3,67},{4,68},{5,69},{6,70},{7,71},{8,72},{9,... | collective-permute-start | bytes 786440 | tf_op jit(solution)/shard_map/ppermute | solution.py:61
  175.0 14.0 %collective-permute-start.31 = (bf16[2,256,256]{2,1,0:T(8,128)(2,1)S(1)}, bf16[2,256,256]{2,1,0:T(8,128)(2,1)S(1)}, u32[]{:S(2)}, u32[]{:S(2)}) collective-permute-start(bf16[2,256,256]{2,1,0:T(8,128)(2,1)S(1)} %get-tuple-element.132), channel_id=1, source_target_pairs={{0,96},{1,97},{2,98},{3,99},{4,100},{5,101},{6,102},{7,103},{8,104... | collective-permute-start | bytes 786440 | tf_op jit(solution)/shard_map/ppermute | solution.py:61
  176.0 13.1 %collective-permute-start.25 = (bf16[2,256,256]{2,1,0:T(8,128)(2,1)S(1)}, bf16[2,256,256]{2,1,0:T(8,128)(2,1)S(1)}, u32[]{:S(2)}, u32[]{:S(2)}) collective-permute-start(bf16[2,256,256]{2,1,0:T(8,128)(2,1)S(1)} %get-tuple-element.127), channel_id=1, source_target_pairs={{0,4},{1,5},{2,6},{3,7},{4,8},{5,9},{6,10},{7,11},{8,12},{9,13},{1... | collective-permute-start | bytes 786440 | tf_op jit(solution)/shard_map/ppermute | solution.py:61
  186.5 7.9 %collective-permute-start.27 = (bf16[2,256,256]{2,1,0:T(8,128)(2,1)S(1)}, bf16[2,256,256]{2,1,0:T(8,128)(2,1)S(1)}, u32[]{:S(2)}, u32[]{:S(2)}) collective-permute-start(bf16[2,256,256]{2,1,0:T(8,128)(2,1)S(1)} %get-tuple-element.128), channel_id=1, source_target_pairs={{0,8},{1,9},{2,10},{3,11},{4,12},{5,13},{6,14},{7,15},{8,0},{9,1},... | collective-permute-start | bytes 786440 | tf_op jit(solution)/shard_map/ppermute | solution.py:61
  186.6 8.5 %collective-permute-start.26 = (bf16[2,256,256]{2,1,0:T(8,128)(2,1)S(1)}, bf16[2,256,256]{2,1,0:T(8,128)(2,1)S(1)}, u32[]{:S(2)}, u32[]{:S(2)}) collective-permute-start(bf16[2,256,256]{2,1,0:T(8,128)(2,1)S(1)} %get-tuple-element.129), channel_id=1, source_target_pairs={{0,12},{1,13},{2,14},{3,15},{4,0},{5,1},{6,2},{7,3},{8,4},{9,5},{1... | collective-permute-start | bytes 786440 | tf_op jit(solution)/shard_map/ppermute | solution.py:61
  195.3 6.5 %collective-permute-start.33 = (bf16[2,256,256]{2,1,0:T(8,128)(2,1)S(1)}, bf16[2,256,256]{2,1,0:T(8,128)(2,1)S(1)}, u32[]{:S(2)}, u32[]{:S(2)}) collective-permute-start(bf16[2,256,256]{2,1,0:T(8,128)(2,1)S(1)} %pad_maximum_fusion.2), channel_id=1, source_target_pairs={{0,16},{1,17},{2,18},{3,19},{4,20},{5,21},{6,22},{7,23},{8,24},{9,... | collective-permute-start | bytes 786440 | tf_op jit(solution)/shard_map/ppermute | solution.py:61
  195.8 1.4 collective-permute-start.40
